TPU v7x, 32 devices: a whole 2x2x4 slice. The times are simulated.
32 devices in a mesh: groups: 2 (over x), seq: 16 (over z, y, core).
Axes of the slice: x: 2, y: 2, z: 4, core: 2. Of those that a mesh axis runs over, the one named last changes fastest.
Arguments:
- streams: bfloat16 [32768, 3, 1024], P(('groups', 'seq')), parts along dimension 0, may hold values from -6 to 6
- short_filter: float32 [3, 3, 1024], replicated, may hold values from -3.5 to 3.5
- residues: float32 [16, 1024], replicated, may hold values from -1.5 to 1.5
- rates: float32 [16, 1024], replicated, may hold values from 6.1035157e-06 to 0.05
- skip: float32 [1024], replicated, may hold values from -1 to 1
Outputs:
- mixed: float32 [32768, 1024], P(('groups', 'seq')), parts along dimension 0
There are 2 independent parts, one for each index of `groups`. A program takes and returns all parts, laid end to end along the dimension named above; an argument that names none is the same for every part. Nothing has to cross between parts.
All inputs are finite; a program needn't handle non-finite values.
Results may differ from a plain program's by a relative error of at most 0.0003.
Values may be sent and summed in bfloat16 or wider, within the bound.
No kernel may reach another device: no remote copies, remote signals or barrier semaphores. Data moves between devices by JAX's collectives and lax.ppermute only.
A program may use at most 192 MiB of HBM per device.

v0:
```python
import jax
import jax.numpy as jnp
from jax import lax
from jax.sharding import PartitionSpec as P

SUB = 64


def from_behind(x, axis, by):
    count = lax.axis_size(axis)
    pairs = [(i, i + by) for i in range(count) if 0 <= i + by < count]
    return lax.ppermute(x, axis, pairs)


def prefix(x, axis, combine, identity):
    count, mine = (lax.axis_size(axis), lax.axis_index(axis))
    everything = jax.tree.map(lambda part: lax.all_gather(part, axis), x)
    start = jax.tree.map(
        lambda part, zero: jnp.broadcast_to(jnp.asarray(zero, part.dtype), part.shape), x, identity
    )

    def step(k, before):
        reached = k < mine
        new = combine(before, jax.tree.map(lambda part: part[k], everything))
        return jax.tree.map(lambda a, b: jnp.where(reached, a, b), new, before)

    return lax.fori_loop(0, count, step, start)


def body(streams, short_filter, residues, rates, skip):
    tok_rows = streams.shape[0]
    channels = streams.shape[2]
    tap_count = short_filter.shape[0]
    highest = lax.Precision.HIGHEST
    rim_rows = from_behind(streams[tok_rows - (tap_count - 1) :], "seq", 1)
    extended = jnp.concatenate([rim_rows, streams], axis=0).astype(jnp.float32)
    filtered = short_filter[0][None] * extended[tap_count - 1 : tap_count - 1 + tok_rows]
    for offset in range(1, tap_count):
        filtered = (
            filtered
            + short_filter[offset][None]
            * extended[tap_count - 1 - offset : tap_count - 1 - offset + tok_rows]
        )
    queries = filtered[:, 0]
    gated_in = filtered[:, 1] * filtered[:, 2]
    coefficient = residues * jnp.sqrt(-jnp.expm1(-2.0 * rates))
    lag_index = jnp.arange(SUB, dtype=jnp.float32)
    decay_lag = jnp.exp(-rates[None] * lag_index[:, None, None])
    kernel = jnp.sum(coefficient[None] * decay_lag, axis=1)
    lag_diff = jnp.arange(SUB, dtype=jnp.int32)[:, None] - jnp.arange(SUB, dtype=jnp.int32)[None, :]
    toeplitz = jnp.where((lag_diff >= 0)[:, :, None], kernel[jnp.clip(lag_diff, 0, SUB - 1)], 0.0)
    num_blocks = tok_rows // SUB
    blocks = gated_in.reshape(num_blocks, SUB, channels)
    inside = jnp.einsum("tsc,bsc->btc", toeplitz, blocks, precision=highest)
    tail_decay = jnp.exp(-rates[None] * (SUB - 1 - lag_index)[:, None, None])
    block_states = jnp.einsum("snc,bsc->bnc", tail_decay, blocks, precision=highest)
    head_decay = coefficient[None] * jnp.exp(-rates[None] * (lag_index + 1.0)[:, None, None])
    step_decay = jnp.exp(-rates * SUB)

    def advance(carried, block_state):
        updated = step_decay * carried + block_state
        return (updated, carried)

    block_end, local_in = lax.scan(advance, jnp.zeros_like(rates), block_states)
    device_decay = jnp.exp(-rates * tok_rows)

    def combine(earlier, latter):
        return (earlier[0] * latter[0], latter[0] * earlier[1] + latter[1])

    identity = (jnp.ones_like(rates), jnp.zeros_like(rates))
    incoming = prefix((device_decay, block_end), "seq", combine, identity)[1]
    block_starts = jnp.arange(num_blocks, dtype=jnp.float32) * SUB
    carry_in = local_in + jnp.exp(-rates[None] * block_starts[:, None, None]) * incoming[None]
    carried_part = jnp.einsum("tnc,bnc->btc", head_decay, carry_in, precision=highest)
    convolved = (inside + carried_part).reshape(tok_rows, channels)
    return queries * (convolved + skip[None] * gated_in)


def solution(mesh):
    placed = (P(("groups", "seq"), None, None), P(), P(), P(), P())
    return jax.shard_map(
        body, mesh=mesh, in_specs=placed, out_specs=P(("groups", "seq"), None), check_vma=False
    )
```

profile of v0, /device:TPU:0, one launch (start us, length us, event | category | flops | bytes accessed | tf_op | source)
XLA Modules:
  0.0 252.5 jit_solution(14828921036283112894)
XLA Ops:
  7.4 2.4 collective-permute-start
  9.8 1.5 multiply_exponential_fusion
  12.7 11.7 %multiply_reduce_fusion = f32[64,1024]{0,1:T(8,128)S(1)} fusion(f32[16,1024]{0,1:T(8,128)S(1)} %copy.23, f32[16,1024]{0,1:T(8,128)S(1)} %copy.22), kind=kLoop, calls=%fused_computation.23 | loop fusion | flops 3080192 | bytes 393216 | tf_op jit(solution)/shard_map/reduce_sum | solution.py:49
  24.6 18.6 %gather_fusion = f32[4096,1024]{1,0:T(8,128)} fusion(f32[64,1024]{1,0:T(8,128)S(1)} %copy.24, s32[4096]{0:T(1024)S(1)} %broadcast_clamp_fusion), kind=kCustom, calls=%fused_computation | custom fusion | bytes 33570816 | tf_op jit(solution)/shard_map/gather | solution.py:51
  43.2 30.5 %copy.25 = f32[64,64,1024]{1,0,2:T(8,128)} copy(f32[64,64,1024]{2,1,0:T(8,128)} %bitcast.52) | data formatting | bytes 33554432 | tf_op jit(solution)/shard_map/gather | solution.py:51
  73.7 4.6 %maximum_convert_fusion = f32[1026,3,1024]{2,0,1:T(8,128)S(1)} fusion(bf16[1024,3,1024]{2,0,1:T(8,128)(2,1)} %param.9, bf16[2,3,1024]{2,0,1:T(2,128)(2,1)S(1)} %collective-permute-done), kind=kLoop, calls=%fused_computation.24 | loop fusion | flops 12607488 | bytes 18911232 | tf_op jit(solution)/shard_map/convert_element_type | solution.py:36
  78.3 6.5 %fusion.5 = f32[1024,3,1024]{2,0,1:T(8,128)} fusion(f32[1026,3,1024]{2,0,1:T(8,128)S(1)} %maximum_convert_fusion, f32[3,1024]{1,0:T(4,128)S(1)} %get-tuple-element.206, f32[3,1024]{1,0:T(4,128)S(1)} %get-tuple-element.207, f32[3,1024]{1,0:T(4,128)S(1)} %get-tuple-element.205), kind=kLoop, calls=%fused_computation.11 | loop fusion | flops 15728640 | bytes 50368512 | tf_op jit(solution)/shard_map/add | solution.py:40
  84.8 6.8 %slice_multiply_fusion.3 = f32[1024,1,1024]{2,0,1:T(8,128)} fusion(f32[1024,3,1024]{2,0,1:T(8,128)} %fusion.5), kind=kLoop, calls=%fused_computation.25 | loop fusion | flops 1048576 | bytes 12582912 | tf_op jit(solution)/shard_map/mul | solution.py:45
  91.6 8.1 %copy.26 = f32[16,64,1024]{1,0,2:T(8,128)} copy(f32[16,64,1024]{2,1,0:T(8,128)} %bitcast.53) | data formatting | bytes 8388608 | tf_op jit(solution)/shard_map/mul | solution.py:45
  99.8 18.2 %fusion.21 = f32[16,16,1024]{1,0,2:T(8,128)} fusion(f32[16,64,1024]{1,0,2:T(8,128)} %copy.26, f32[64]{0:T(128)S(1)} %iota_subtract_fusion, f32[16,1024]{0,1:T(8,128)S(1)} %copy.23), kind=kOutput, calls=%fused_computation.35 | convolution fusion | flops 202375168 | bytes 5308672 | tf_op jit(solution)/shard_map/snc,bsc->bnc/dot_general | solution.py:56
  118.0 5.1 %copy.28 = f32[16,16,1024]{2,1,0:T(8,128)S(1)} copy(f32[16,16,1024]{1,0,2:T(8,128)} %fusion.21) | data formatting | bytes 2097152
  123.1 10.6 %while.27 = (s32[]{:T(128)}, f32[16,1024]{1,0:T(8,128)S(1)}, f32[16,16,1024]{2,1,0:T(8,128)}, f32[16,1024]{1,0:T(8,128)S(1)}, f32[16,16,1024]{2,1,0:T(8,128)S(1)}, /*index=5*/s32[]{:T(128)}, s32[]{:T(128)}) while((s32[]{:T(128)}, f32[16,1024]{1,0:T(8,128)S(1)}, f32[16,16,1024]{2,1,0:T(8,128)}, f32[16,1024]{1,0:T(8,128)S(1)}, ...), condition=%wide.region_2.3_spmd.clone, body=%wide.region_1.2_spmd.clone.sunk | while | flops 65539 | bytes 393320 | solution.py:64
  134.5 57.4 %fusion.1 = f32[1024,16,64]{2,1,0:T(8,128)} fusion(f32[16,64,1024]{1,0,2:T(8,128)} %copy.26, f32[64,64,1024]{1,0,2:T(8,128)} %copy.25, pred[64,64]{1,0:T(8,128)(4,1)S(1)} %subtract_compare_fusion), kind=kOutput, calls=%fused_computation.6 | convolution fusion | flops 809500672 | bytes 25169920 | tf_op jit(solution)/shard_map/tsc,bsc->btc/dot_general | solution.py:54
  191.9 15.0 %while.28 = (s32[]{:T(128)}, f32[16,1024]{1,0:T(8,128)S(1)}, s32[]{:T(128)}, f32[16,16,1024]{2,1,0:T(8,128)}, f32[16,16,1024]{2,1,0:T(8,128)}, /*index=5*/s32[]{:T(128)}, s32[]{:T(128)}) while((s32[]{:T(128)}, f32[16,1024]{1,0:T(8,128)S(1)}, s32[]{:T(128)}, f32[16,16,1024]{2,1,0:T(8,128)}, f32[16,16,1024]{2,1,0:T(8,128)}, ...), condition=%wide.region_4.5_spmd.clone, body=%wide.region_3.4_spmd.clone.sunk | while | flops 65540 | bytes 262253 | solution.py:27
  192.8 0.9 fusion.34
  193.7 0.9 fusion.34
  194.7 0.9 fusion.34
  195.6 0.9 fusion.34
  197.5 0.9 fusion.34
  204.0 0.9 fusion.34
  207.1 6.2 %copy.29 = f32[16,16,1024]{1,0,2:T(8,128)} copy(f32[16,16,1024]{2,1,0:T(8,128)S(1)} %multiply_add_fusion) | data formatting | bytes 2097152 | tf_op jit(solution)/shard_map/add | solution.py:73
  213.3 15.1 %add_bitcast_fusion = f32[16,64,1024]{1,0,2:T(8,128)} fusion(f32[1024,16,64]{2,1,0:T(8,128)} %fusion.1, f32[16,16,1024]{1,0,2:T(8,128)} %copy.29, f32[64]{0:T(128)S(1)} %iota_add_fusion, f32[16,1024]{0,1:T(8,128)S(1)} %copy.23, f32[16,1024]{0,1:T(8,128)S(1)} %copy.22), kind=kOutput, calls=%fused_computation.15 | convolution fusion | flops 204472320 | bytes 9568512 | tf_op jit(solution)/shard_map/tnc,bnc->btc/dot_general | solution.py:74
  228.4 6.9 %copy.30 = f32[16,64,1024]{2,1,0:T(8,128)} copy(f32[16,64,1024]{1,0,2:T(8,128)} %add_bitcast_fusion) | data formatting | bytes 8388608 | tf_op jit(solution)/shard_map/add | solution.py:75
  235.3 10.4 %fusion.14 = f32[1024,1024]{1,0:T(8,128)} fusion(f32[1024,3,1024]{2,0,1:T(8,128)} %fusion.5, f32[16,64,1024]{2,1,0:T(8,128)} %copy.30, f32[1024]{0:T(1024)S(1)} %copy-done.2), kind=kLoop, calls=%fused_computation.27 | loop fusion | flops 4194304 | bytes 20975616 | tf_op jit(solution)/shard_map/mul | solution.py:76
  (71 shorter events, 22.7 us)
Async XLA Ops:
  6.5 185.3 %all-gather.5.cloned.1.call-start = ((), (), s32[]{:S(2)}) async-start(), calls=%async_computation | async-start | bytes 1114112 | tf_op jit(solution)/shard_map/all_gather | solution.py:17
  7.4 66.3 %collective-permute-start = (bf16[2,3,1024]{2,0,1:T(2,128)(2,1)S(1)}, bf16[2,3,1024]{2,0,1:T(2,128)(2,1)S(1)}, u32[]{:S(2)}, u32[]{:S(2)}) collective-permute-start(bf16[2,3,1024]{2,0,1:T(2,128)(2,1)S(1)} %slice.31), channel_id=1, source_target_pairs={{0,1},{1,2},{2,3},{3,4},{4,5},{5,6},{6,7},{7,8},{8,9},{9,10},{10,1... | collective-permute-start | bytes 36872 | tf_op jit(solution)/shard_map/ppermute | solution.py:12
  11.3 180.5 %all-gather.7.cloned.1.call-start = ((), (), s32[]{:S(2)}) async-start(), calls=%async_computation.1 | async-start | bytes 1114112 | tf_op jit(solution)/shard_map/all_gather | solution.py:17
  133.7 0.6 copy-start
  134.4 72.4 %copy-start.1 = (f32[16,16,1024]{2,1,0:T(8,128)S(1)}, f32[16,16,1024]{2,1,0:T(8,128)}, u32[]{:S(2)}) copy-start(f32[16,16,1024]{2,1,0:T(8,128)} %get-tuple-element.127) | copy-start | bytes 3145732
  228.4 6.9 %copy-start.2 = (f32[1024]{0:T(1024)S(1)}, f32[1024]{0:T(1024)}, u32[]{:S(2)}) copy-start(f32[1024]{0:T(1024)} %param.13) | copy-start | bytes 12292
Sparse Core Ops, SparseCore 0:
  11.4 40.4 all-gather.4
  134.5 40.4 all-gather.6
where the time goes:
time: 257 us; the launch traced here: 253 us
  matrix products  90.7 us (35%)
  local copies, waits for them, and re-layouts  78.2 us (30%)
  other arithmetic  66.9 us (26%)
  between operations  13.6 us (5%)
    dot_general x1, matrix products, body(): inside = jnp.einsum('tsc,bsc->btc', toeplitz, blocks, precision=highest)  57.4 us
    gather x2, local copies, waits for them, and re-layouts, body(): kernel[jnp.clip(lag_diff, 0, SUB - 1)]  49.1 us
    dot_general x1, matrix products, body(): jnp.einsum('snc,bsc->bnc', tail_decay, blocks, precision=highest)  18.2 us
    dot_general x1, matrix products, body(): jnp.einsum('tnc,bnc->btc', head_decay, carry_in, precision=highest)  15.1 us
    select_n x16, other arithmetic, step(): return jax.tree.map(lambda a, b: jnp.where(reached, a, b), new, before)  14.6 us
    reduce_sum x1, other arithmetic, body(): kernel = jnp.sum(coefficient[None] * decay_lag, axis=1)  11.7 us
    mul x1, other arithmetic, body(): return queries * (convolved + skip[None] * gated_in)  10.4 us
    dynamic_update_slice x16, other arithmetic, body(): block_end, local_in = lax.scan(advance, jnp.zeros_like(rates), block_states)  10 us
  transfers between devices with their start and end apart: 3, of which 0 were waited for; matrix products, arithmetic and copies ran while one was open for 72% of the time, Pallas kernels for 0%

commit v1 on v0

v1 whole, which is shorter than its diff:
```python
import functools

import jax
import jax.numpy as jnp
from jax import lax
from jax.experimental import pallas as pl
from jax.experimental.pallas import tpu as pltpu
from jax.sharding import PartitionSpec as P

SEG = 8
LANES = 128
PAD = 8
UNROLL = 8
f32 = jnp.float32


def rows(vec):
    return jnp.broadcast_to(vec, (SEG, LANES))


def total(parts):
    while len(parts) > 1:
        tail = [parts[-1]] if len(parts) % 2 else []
        parts = [a + b for a, b in zip(parts[::2], parts[1::2])] + tail
    return parts[0]


def later(x, by, fill):
    row = lax.broadcasted_iota(jnp.int32, x.shape, 0)
    return jnp.where(row >= by, pltpu.roll(x, by, 0), fill)


def spread(src, dst, steps):
    def one(i, _):
        here = pl.ds(pl.multiple_of(i * steps, 16), steps)
        there = pl.ds(pl.multiple_of(i * (steps + PAD), 8), steps)
        dst[there, :] = src[here, :].astype(f32)
        return 0

    lax.fori_loop(0, SEG, one, 0)
    return lambda k: dst[pl.ds(k, SEG, stride=steps + PAD), :]


def scan_steps(steps, one, start):
    def some(b, c):
        for u in range(UNROLL):
            c = one(b * UNROLL + u, c)
        return c

    return lax.fori_loop(0, steps // UNROLL, some, start)


def states_kernel(key_ref, val_ref, rim_ref, tap_ref, rate_ref, gated_ref, start_ref, end_ref, keys, vals):
    steps = key_ref.shape[0] // SEG
    modes = rate_ref.shape[0]
    at = [spread(key_ref, keys, steps), spread(val_ref, vals, steps)]
    taps = [[rows(tap_ref[d, j : j + 1, :]) for d in range(3)] for j in (1, 2)]
    decay = [rows(jnp.exp(-rate_ref[n : n + 1, :])) for n in range(modes)]
    before = []
    for j in range(2):
        before.append(later(at[j](steps - 1), 1, rim_ref[j + 1, 1:2, :]))
        before.append(later(at[j](steps - 2), 1, rim_ref[j + 1, 0:1, :]))

    def one(k, c):
        k1, k2, v1, v2, *state = c
        k0, v0 = at[0](k), at[1](k)
        a = taps[0][0] * k0 + taps[0][1] * k1 + taps[0][2] * k2
        b = taps[1][0] * v0 + taps[1][1] * v1 + taps[1][2] * v2
        x = a * b
        gated_ref[k] = x
        return (k0, k1, v0, v1, *[d * s + x for d, s in zip(decay, state)])

    zero = jnp.zeros((SEG, LANES), f32)
    final = scan_steps(steps, one, (*before, *[zero] * modes))[4:]
    for n in range(modes):
        s = final[n]
        d = rows(jnp.exp(-rate_ref[n : n + 1, :] * steps))
        for by in (1, 2, 4):
            s = s + d * later(s, by, 0.0)
            d = d * d
        start_ref[n] = later(s, 1, 0.0)
        end_ref[n : n + 1, :] = s[SEG - 1 : SEG, :]


def local_kernel(query_ref, gated_ref, rim_ref, tap_ref, rate_ref, coef_ref, skip_ref, start_ref, conv_ref, gate_ref, queries):
    steps = query_ref.shape[0] // SEG
    modes = rate_ref.shape[0]
    at = spread(query_ref, queries, steps)
    taps = [rows(tap_ref[d, 0:1, :]) for d in range(3)]
    decay = [rows(jnp.exp(-rate_ref[n : n + 1, :])) for n in range(modes)]
    coef = [rows(coef_ref[n : n + 1, :]) for n in range(modes)]
    skip = rows(skip_ref[...])
    before = (later(at(steps - 1), 1, rim_ref[0, 1:2, :]), later(at(steps - 2), 1, rim_ref[0, 0:1, :]))

    def one(k, c):
        q1, q2, *state = c
        q0, x = at(k), gated_ref[k]
        gate_ref[k] = taps[0] * q0 + taps[1] * q1 + taps[2] * q2
        state = [d * s + x for d, s in zip(decay, state)]
        conv_ref[k] = total([a * s for a, s in zip(coef, state)] + [skip * x])
        return (q0, q1, *state)

    scan_steps(steps, one, (*before, *[start_ref[n] for n in range(modes)]))


def carry_kernel(conv_ref, gate_ref, rate_ref, carry_ref, out_ref, mixed):
    steps = conv_ref.shape[0]
    modes = rate_ref.shape[0]
    decay = [rows(jnp.exp(-rate_ref[n : n + 1, :])) for n in range(modes)]
    first = lax.broadcasted_iota(jnp.int32, (SEG, LANES), 0).astype(f32) * steps
    part = [jnp.exp(-rate_ref[n : n + 1, :] * first) * carry_ref[n : n + 1, :] for n in range(modes)]

    def one(k, part):
        part = [d * s for d, s in zip(decay, part)]
        mixed[pl.ds(k, SEG, stride=steps + PAD), :] = gate_ref[k] * (conv_ref[k] + total(part))
        return part

    scan_steps(steps, one, part)

    def gather(i, _):
        there = pl.ds(pl.multiple_of(i * (steps + PAD), 8), steps)
        out_ref[pl.ds(pl.multiple_of(i * steps, 8), steps), :] = mixed[there, :]
        return 0

    lax.fori_loop(0, SEG, gather, 0)


def body(streams, short_filter, residues, rates, skip):
    tokens, _, channels = streams.shape
    modes = rates.shape[0]
    steps = tokens // SEG
    count, mine = lax.axis_size("seq"), lax.axis_index("seq")
    assert count & (count - 1) == 0 and tokens % (SEG * 16) == 0

    rim = lax.ppermute(streams[tokens - 2 :], "seq", [(i, i + 1) for i in range(count - 1)])
    rim = jnp.transpose(rim, (1, 0, 2)).astype(f32)
    by_stream = jnp.transpose(streams, (1, 0, 2))
    coefficient = residues * jnp.sqrt(-jnp.expm1(-2.0 * rates))

    def stream(j):
        return pl.BlockSpec((None, tokens, LANES), lambda c: (j, 0, c))

    grid = (channels // LANES,)
    segs = pl.BlockSpec((steps, SEG, LANES), lambda c: (0, 0, c))
    rims = pl.BlockSpec((3, 2, LANES), lambda c: (0, 0, c))
    taps = pl.BlockSpec((3, 3, LANES), lambda c: (0, 0, c))
    mode = pl.BlockSpec((modes, LANES), lambda c: (0, c))
    mode_segs = pl.BlockSpec((modes, SEG, LANES), lambda c: (0, 0, c))
    padded = pltpu.VMEM((SEG * (steps + PAD), LANES), f32)
    seg_shape = jax.ShapeDtypeStruct((steps, SEG, channels), f32)

    gated, starts, end = pl.pallas_call(
        states_kernel,
        grid=grid,
        in_specs=[stream(1), stream(2), rims, taps, mode],
        out_specs=[segs, mode_segs, mode],
        out_shape=[
            seg_shape,
            jax.ShapeDtypeStruct((modes, SEG, channels), f32),
            jax.ShapeDtypeStruct((modes, channels), f32),
        ],
        scratch_shapes=[padded, padded],
        name="states",
    )(by_stream, by_stream, rim, short_filter, rates)

    block, entering = end, jnp.zeros_like(end)
    size = 1
    while size < count:
        other = lax.ppermute(block, "seq", [(i, i ^ size) for i in range(count)])
        second = (mine & size) != 0
        behind = (mine & (size - 1)).astype(f32) * tokens
        entering = jnp.where(second, entering + jnp.exp(-rates * behind) * other, entering)
        across = jnp.exp(-rates * float(tokens * size))
        block = jnp.where(second, block + across * other, other + across * block)
        size *= 2

    conv, gate = pl.pallas_call(
        local_kernel,
        grid=grid,
        in_specs=[stream(0), segs, rims, taps, mode, mode, pl.BlockSpec((1, LANES), lambda c: (0, c)), mode_segs],
        out_specs=[segs, segs],
        out_shape=[seg_shape, seg_shape],
        scratch_shapes=[padded],
        name="local",
    )(by_stream, gated, rim, short_filter, rates, coefficient, skip[None], starts)

    return pl.pallas_call(
        carry_kernel,
        grid=grid,
        in_specs=[segs, segs, mode, mode],
        out_specs=pl.BlockSpec((tokens, LANES), lambda c: (0, c)),
        out_shape=jax.ShapeDtypeStruct((tokens, channels), f32),
        scratch_shapes=[padded],
        name="carry",
    )(conv, gate, rates, coefficient * entering)


def solution(mesh):
    placed = (P(("groups", "seq"), None, None), P(), P(), P(), P())
    return jax.shard_map(
        body, mesh=mesh, in_specs=placed, out_specs=P(("groups", "seq"), None), check_vma=False
    )
```

time: 257 us -> 63.3 us (0.25); the launches traced: 253 us -> 62.7 us
  matrix products: 90.7 us -> 0 us
  local copies, waits for them, and re-layouts: 78.2 us -> 0.82 us
  other arithmetic: 66.9 us -> 2.29 us
  Pallas kernels: 0 us -> 37.1 us
  between operations: 13.6 us -> 0.03 us
  starting transfers between devices: 2.44 us -> 13.6 us
  waiting for transfers between devices: 0.04 us -> 8.83 us
    dot_general x3 -> x0, matrix products: 90.7 us -> none  [the longest x1 57.4 us: body(): inside = jnp.einsum('tsc,bsc->btc', toeplitz, blocks, precision=highest)]
    gather x2 -> x0, local copies, waits for them, and re-layouts: 49.1 us -> none  [body(): kernel[jnp.clip(lag_diff, 0, SUB - 1)]]
    pallas_call x0 -> x3, Pallas kernels: none -> 37.1 us  [the longest x1 15.2 us: body(): pl.pallas_call(local_kernel, grid=grid, in_specs=[stream(0), segs, rims,...]
    mul x3 -> x1, other arithmetic: 17.2 us -> 0.76 us  [body(): coefficient * entering]
    select_n x17 -> x3, other arithmetic: 14.7 us -> 0.92 us  [body(): block = jnp.where(second, block + across * other, other + across * block)]
    add x2 -> x0, local copies, waits for them, and re-layouts: 13.1 us -> none  [the longest x1 6.88 us: body(): convolved = (inside + carried_part).reshape(tok_rows, channels)]
    reduce_sum x1 -> x0, other arithmetic: 11.7 us -> none  [body(): kernel = jnp.sum(coefficient[None] * decay_lag, axis=1)]
    ppermute x1 -> x5, starting transfers between devices: 2.4 us -> 13.6 us  [the longest x4 11.2 us: body(): other = lax.ppermute(block, 'seq', [(i, i ^ size) for i in range(count)])]
  transfers between devices with their start and end apart: 3 -> 5, of which waited for: 0 -> 5; matrix products, arithmetic and copies ran while one was open for 72% -> 0% of each run, Pallas kernels for 0% -> 0%
where the time goes in v1:
time: 63.3 us; the launch traced here: 62.7 us
  Pallas kernels  37.1 us (59%)
  starting transfers between devices  13.6 us (21%)
  waiting for transfers between devices  8.83 us (14%)
  other arithmetic  2.29 us (4%)
  local copies, waits for them, and re-layouts  0.82 us (1%)
    pallas_call x1, Pallas kernels, body(): pl.pallas_call(local_kernel, grid=grid, in_specs=[stream(0), segs, rims,...  15.2 us
    pallas_call x1, Pallas kernels, body(): pl.pallas_call(states_kernel, grid=grid, in_specs=[stream(1), stream(2),...  11.7 us
    ppermute x4, starting transfers between devices, body(): other = lax.ppermute(block, 'seq', [(i, i ^ size) for i in range(count)])  11.2 us
    pallas_call x1, Pallas kernels, body(): pl.pallas_call(carry_kernel, grid=grid, in_specs=[segs, segs, mode, mode]...  10.2 us
    ppermute x4, waiting for transfers between devices, body(): other = lax.ppermute(block, 'seq', [(i, i ^ size) for i in range(count)])  8.02 us
    ppermute x1, starting transfers between devices, body(): lax.ppermute(streams[tokens - 2:], 'seq', [(i, i + 1) for i in range(coun...  2.4 us
  transfers between devices with their start and end apart: 5, of which 5 were waited for; matrix products, arithmetic and copies ran while one was open for 0% of the time, Pallas kernels for 0%

profile of v1, /device:TPU:0, one launch (start us, length us, event | category | flops | bytes accessed | tf_op | source)
XLA Modules:
  0.0 62.7 jit_solution(8264011423427904099)
XLA Ops:
  0.0 0.8 %slice.3 = bf16[2,3,1024]{2,0,1:T(2,128)(2,1)S(1)} slice(bf16[1024,3,1024]{2,0,1:T(8,128)(2,1)} %param.5), slice={[1022:1024], [0:3], [0:1024]} | slice | bytes 24576 | tf_op jit(solution)/shard_map/slice | solution.py:135
  0.8 2.4 %collective-permute-start = (bf16[2,3,1024]{2,0,1:T(2,128)(2,1)S(1)}, bf16[2,3,1024]{2,0,1:T(2,128)(2,1)S(1)}, u32[]{:S(2)}, u32[]{:S(2)}) collective-permute-start(bf16[2,3,1024]{2,0,1:T(2,128)(2,1)S(1)} %slice.3), channel_id=1, source_target_pairs={{0,1},{1,2},{2,3},{3,4},{4,5},{5,6},{6,7},{7,8},{8,9},{9,10},{10,1... | collective-permute-start | bytes 36872 | tf_op jit(solution)/shard_map/ppermute | solution.py:135
  3.2 0.8 %collective-permute-done = bf16[2,3,1024]{2,0,1:T(2,128)(2,1)S(1)} collective-permute-done((bf16[2,3,1024]{2,0,1:T(2,128)(2,1)S(1)}, bf16[2,3,1024]{2,0,1:T(2,128)(2,1)S(1)}, u32[]{:S(2)}, u32[]{:S(2)}) %collective-permute-start) | collective-permute-done | bytes 12320 | tf_op jit(solution)/shard_map/ppermute | solution.py:135
  4.0 0.6 convert_bitcast_fusion.rim_ref
  4.7 0.0 copy-start
  4.7 0.0 copy-start.1
  4.7 11.7 %states.1 = (f32[128,8,1024]{2,1,0:T(8,128)}, f32[16,8,1024]{2,1,0:T(8,128)}, f32[16,1024]{1,0:T(8,128)}) custom-call(bf16[3,1024,1024]{2,1,0:T(8,128)(2,1)} %bitcast.4, bf16[3,1024,1024]{2,1,0:T(8,128)(2,1)} %bitcast.5, f32[3,2,1024]{2,1,0:T(2,128)} %convert_bitcast_fusion.rim_ref, f32[3,3,1024]{2,1,0:T(4,128)} %tap_ref.3, f32[16,1024]{1,0:T(8,128)} %rate_ref.5), custom_call_target="tpu_custom_call" | custom-call | tf_op jit(solution)/shard_map/states/pallas_call | solution.py:152
  16.4 2.6 %collective-permute-start.1 = (f32[16,1024]{1,0:T(8,128)}, f32[16,1024]{1,0:T(8,128)S(1)}, u32[]{:S(2)}, u32[]{:S(2)}) collective-permute-start(f32[16,1024]{1,0:T(8,128)} %get-tuple-element.14), channel_id=1, source_target_pairs={{0,1},{1,0},{2,3},{3,2},{4,5},{5,4},{6,7},{7,6},{8,9},{9,8},{10,11... | collective-permute-start | bytes 196616 | tf_op jit(solution)/shard_map/ppermute | solution.py:169
  19.0 1.1 %collective-permute-done.1 = f32[16,1024]{1,0:T(8,128)S(1)} collective-permute-done((f32[16,1024]{1,0:T(8,128)}, f32[16,1024]{1,0:T(8,128)S(1)}, u32[]{:S(2)}, u32[]{:S(2)}) %collective-permute-start.1) | collective-permute-done | bytes 65568 | tf_op jit(solution)/shard_map/ppermute | solution.py:169
  20.1 0.0 copy-done
  20.1 0.9 %add_select_fusion.5 = f32[16,1024]{1,0:T(8,128)S(1)} fusion(f32[16,1024]{1,0:T(8,128)S(1)} %collective-permute-done.1, f32[16,1024]{1,0:T(8,128)} %get-tuple-element.14, f32[16,1024]{1,0:T(8,128)S(1)} %copy-done, pred[]{:T(512)S(6)} %ne.15), kind=kLoop, calls=%fused_computation.6 | loop fusion | flops 114688 | bytes 262145 | tf_op jit(solution)/shard_map/jit(_where)/select_n | solution.py:174
  21.0 2.6 %collective-permute-start.2 = (f32[16,1024]{1,0:T(8,128)S(1)}, f32[16,1024]{1,0:T(8,128)S(1)}, u32[]{:S(2)}, u32[]{:S(2)}) collective-permute-start(f32[16,1024]{1,0:T(8,128)S(1)} %add_select_fusion.5), channel_id=1, source_target_pairs={{0,2},{1,3},{2,0},{3,1},{4,6},{5,7},{6,4},{7,5},{8,10},{9,11},{10,... | collective-permute-start | bytes 196616 | tf_op jit(solution)/shard_map/ppermute | solution.py:169
  23.6 2.4 %collective-permute-done.2 = f32[16,1024]{1,0:T(8,128)S(1)} collective-permute-done((f32[16,1024]{1,0:T(8,128)S(1)}, f32[16,1024]{1,0:T(8,128)S(1)}, u32[]{:S(2)}, u32[]{:S(2)}) %collective-permute-start.2) | collective-permute-done | bytes 65568 | tf_op jit(solution)/shard_map/ppermute | solution.py:169
  26.0 2.9 %collective-permute-start.3 = (f32[16,1024]{1,0:T(8,128)S(1)}, f32[16,1024]{1,0:T(8,128)S(1)}, u32[]{:S(2)}, u32[]{:S(2)}) collective-permute-start(f32[16,1024]{1,0:T(8,128)S(1)} %add_select_fusion.4), channel_id=1, source_target_pairs={{0,4},{1,5},{2,6},{3,7},{4,0},{5,1},{6,2},{7,3},{8,12},{9,13},{10,... | collective-permute-start | bytes 196616 | tf_op jit(solution)/shard_map/ppermute | solution.py:169
  28.9 2.2 %collective-permute-done.3 = f32[16,1024]{1,0:T(8,128)S(1)} collective-permute-done((f32[16,1024]{1,0:T(8,128)S(1)}, f32[16,1024]{1,0:T(8,128)S(1)}, u32[]{:S(2)}, u32[]{:S(2)}) %collective-permute-start.3) | collective-permute-done | bytes 65568 | tf_op jit(solution)/shard_map/ppermute | solution.py:169
  31.2 3.1 %collective-permute-start.4 = (f32[16,1024]{1,0:T(8,128)S(1)}, f32[16,1024]{1,0:T(8,128)S(1)}, u32[]{:S(2)}, u32[]{:S(2)}) collective-permute-start(f32[16,1024]{1,0:T(8,128)S(1)} %add_select_fusion.3), channel_id=1, source_target_pairs={{0,8},{1,9},{2,10},{3,11},{4,12},{5,13},{6,14},{7,15},{8,0},{9,1},... | collective-permute-start | bytes 196616 | tf_op jit(solution)/shard_map/ppermute | solution.py:169
  34.3 2.2 %collective-permute-done.4 = f32[16,1024]{1,0:T(8,128)S(1)} collective-permute-done((f32[16,1024]{1,0:T(8,128)S(1)}, f32[16,1024]{1,0:T(8,128)S(1)}, u32[]{:S(2)}, u32[]{:S(2)}) %collective-permute-start.4) | collective-permute-done | bytes 65568 | tf_op jit(solution)/shard_map/ppermute | solution.py:169
  36.5 0.0 copy-done.1
  36.5 0.8 %fusion = (f32[16,1024]{1,0:T(8,128)}, f32[16,1024]{1,0:T(8,128)}) fusion(f32[16,1024]{1,0:T(8,128)S(1)} %collective-permute-done.4, f32[16,1024]{1,0:T(8,128)S(1)} %collective-permute-done.3, f32[16,1024]{1,0:T(8,128)S(1)} %collective-permute-done.2, f32[16,1024]{1,0:T(8,128)S(1)} %collective-permute-done.1, f32[16,1024]{1,0:T(8,128)S(1)} %copy-done, ...), kind=kLoop, calls=%fused_computation.3 | loop fusion | flops 327680 | bytes 524304 | tf_op jit(solution)/shard_map/mul | solution.py:195
  37.3 15.2 %local.1 = (f32[128,8,1024]{2,1,0:T(8,128)}, f32[128,8,1024]{2,1,0:T(8,128)}) custom-call(bf16[3,1024,1024]{2,1,0:T(8,128)(2,1)} %bitcast.6, f32[128,8,1024]{2,1,0:T(8,128)} %get-tuple-element.10.gated_ref, f32[3,2,1024]{2,1,0:T(2,128)} %convert_bitcast_fusion.rim_ref, f32[3,3,1024]{2,1,0:T(4,128)} %tap_ref.3, f32[16,1024]{1,0:T(8,128)} %rate_ref.5, ...), custom_call_target="tpu_custom_call" | custom-call | tf_op jit(solution)/shard_map/local/pallas_call | solution.py:177
  52.4 10.2 %carry.1 = f32[1024,1024]{1,0:T(8,128)} custom-call(f32[128,8,1024]{2,1,0:T(8,128)} %get-tuple-element.12.conv_ref, f32[128,8,1024]{2,1,0:T(8,128)} %get-tuple-element.13.gate_ref, f32[16,1024]{1,0:T(8,128)} %rate_ref.5, f32[16,1024]{1,0:T(8,128)} %get-tuple-element.15.carry_ref), custom_call_target="tpu_custom_call" | custom-call | tf_op jit(solution)/shard_map/carry/pallas_call | solution.py:187
  (2 shorter events, 0.1 us)
Async XLA Ops:
  0.8 3.2 %collective-permute-start = (bf16[2,3,1024]{2,0,1:T(2,128)(2,1)S(1)}, bf16[2,3,1024]{2,0,1:T(2,128)(2,1)S(1)}, u32[]{:S(2)}, u32[]{:S(2)}) collective-permute-start(bf16[2,3,1024]{2,0,1:T(2,128)(2,1)S(1)} %slice.3), channel_id=1, source_target_pairs={{0,1},{1,2},{2,3},{3,4},{4,5},{5,6},{6,7},{7,8},{8,9},{9,10},{10,1... | collective-permute-start | bytes 36872 | tf_op jit(solution)/shard_map/ppermute | solution.py:135
  4.7 15.4 %copy-start = (f32[16,1024]{1,0:T(8,128)S(1)}, f32[16,1024]{1,0:T(8,128)}, u32[]{:S(2)}) copy-start(f32[16,1024]{1,0:T(8,128)} %rate_ref.5) | copy-start | bytes 196612
  4.7 31.8 %copy-start.1 = (f32[16,1024]{1,0:T(8,128)S(1)}, f32[16,1024]{1,0:T(8,128)}, u32[]{:S(2)}) copy-start(f32[16,1024]{1,0:T(8,128)} %param.7) | copy-start | bytes 196612
  16.4 3.7 %collective-permute-start.1 = (f32[16,1024]{1,0:T(8,128)}, f32[16,1024]{1,0:T(8,128)S(1)}, u32[]{:S(2)}, u32[]{:S(2)}) collective-permute-start(f32[16,1024]{1,0:T(8,128)} %get-tuple-element.14), channel_id=1, source_target_pairs={{0,1},{1,0},{2,3},{3,2},{4,5},{5,4},{6,7},{7,6},{8,9},{9,8},{10,11... | collective-permute-start | bytes 196616 | tf_op jit(solution)/shard_map/ppermute | solution.py:169
  21.0 5.0 %collective-permute-start.2 = (f32[16,1024]{1,0:T(8,128)S(1)}, f32[16,1024]{1,0:T(8,128)S(1)}, u32[]{:S(2)}, u32[]{:S(2)}) collective-permute-start(f32[16,1024]{1,0:T(8,128)S(1)} %add_select_fusion.5), channel_id=1, source_target_pairs={{0,2},{1,3},{2,0},{3,1},{4,6},{5,7},{6,4},{7,5},{8,10},{9,11},{10,... | collective-permute-start | bytes 196616 | tf_op jit(solution)/shard_map/ppermute | solution.py:169
  26.0 5.1 %collective-permute-start.3 = (f32[16,1024]{1,0:T(8,128)S(1)}, f32[16,1024]{1,0:T(8,128)S(1)}, u32[]{:S(2)}, u32[]{:S(2)}) collective-permute-start(f32[16,1024]{1,0:T(8,128)S(1)} %add_select_fusion.4), channel_id=1, source_target_pairs={{0,4},{1,5},{2,6},{3,7},{4,0},{5,1},{6,2},{7,3},{8,12},{9,13},{10,... | collective-permute-start | bytes 196616 | tf_op jit(solution)/shard_map/ppermute | solution.py:169
  31.2 5.3 %collective-permute-start.4 = (f32[16,1024]{1,0:T(8,128)S(1)}, f32[16,1024]{1,0:T(8,128)S(1)}, u32[]{:S(2)}, u32[]{:S(2)}) collective-permute-start(f32[16,1024]{1,0:T(8,128)S(1)} %add_select_fusion.3), channel_id=1, source_target_pairs={{0,8},{1,9},{2,10},{3,11},{4,12},{5,13},{6,14},{7,15},{8,0},{9,1},... | collective-permute-start | bytes 196616 | tf_op jit(solution)/shard_map/ppermute | solution.py:169

commit v2 on v1

v2 whole, which is shorter than its diff:
```python
import functools

import jax
import jax.numpy as jnp
from jax import lax
from jax.experimental import pallas as pl
from jax.experimental.pallas import tpu as pltpu
from jax.sharding import PartitionSpec as P


SEG = 8
LANES = 128
CHUNK = 16
PITCH = CHUNK + 8
VMEM_LIMIT = 16 << 20
f32 = jnp.float32


def rows(vec):
    return jnp.broadcast_to(vec, (SEG, LANES))


def total(parts):
    while len(parts) > 1:
        tail = [parts[-1]] if len(parts) % 2 else []
        parts = [a + b for a, b in zip(parts[::2], parts[1::2])] + tail
    return parts[0]


def later(x, by):
    row = lax.broadcasted_iota(jnp.int32, x.shape, 0)
    return jnp.where(row >= by, pltpu.roll(x, by, 0), 0.0)


def decays(rate_ref, times):
    return [rows(jnp.exp(-rate_ref[n : n + 1, :] * times)) for n in range(rate_ref.shape[0])]


class Spread:
    def __init__(self, block, slots, steps):
        self.block, self.slots, self.steps = block, slots, steps

    def load(self, seg, chunk, slot):
        start = pl.multiple_of(seg * self.steps + chunk * CHUNK, CHUNK)
        piece = self.block[pl.ds(start, CHUNK), :].astype(f32)
        self.slots[slot, pl.ds(seg * PITCH, CHUNK), :] = piece

    def load_all(self, chunk, slot):
        for seg in range(SEG):
            self.load(seg, chunk, slot)

    def at(self, slot, k):
        return self.slots[slot, pl.ds(k, SEG, stride=PITCH), :]


def chunk_loop(steps, one, ahead, start):
    chunks = steps // CHUNK

    def trip(b, c):
        slot, after = lax.rem(b, 2), lax.rem(b + 1, 2)
        coming = lax.rem(b + 1, chunks)
        for u in range(CHUNK):
            c = one(b * CHUNK + u, slot, u, c)
            ahead(u, b, coming, after)
        return c

    return lax.fori_loop(0, chunks, trip, start)


def states_kernel(key_ref, val_ref, tap_ref, rate_ref, gated_ref, start_ref, end_ref, key_slots, val_slots):
    steps = key_ref.shape[0] // SEG
    modes = rate_ref.shape[0]
    keys, vals = Spread(key_ref, key_slots, steps), Spread(val_ref, val_slots, steps)
    taps = [[rows(tap_ref[d, j : j + 1, :]) for d in range(3)] for j in (1, 2)]
    decay = decays(rate_ref, 1.0)
    before = []
    for part in (keys, vals):
        part.load_all(steps // CHUNK - 1, 1)
        part.load_all(0, 0)
        before += [later(part.at(1, CHUNK - 1), 1), later(part.at(1, CHUNK - 2), 1)]

    def one(k, slot, u, c):
        k1, k2, v1, v2, *state = c
        k0, v0 = keys.at(slot, u), vals.at(slot, u)
        a = taps[0][0] * k0 + taps[0][1] * k1 + taps[0][2] * k2
        b = taps[1][0] * v0 + taps[1][1] * v1 + taps[1][2] * v2
        x = a * b
        gated_ref[k] = x
        return (k0, k1, v0, v1, *[d * s + x for d, s in zip(decay, state)])

    def ahead(u, b, coming, after):
        (keys, vals)[u % 2].load(u // 2, coming, after)

    zero = jnp.zeros((SEG, LANES), f32)
    final = chunk_loop(steps, one, ahead, (*before, *[zero] * modes))[4:]
    for n, d in enumerate(decays(rate_ref, float(steps))):
        s = final[n]
        for by in (1, 2, 4):
            s = s + d * later(s, by)
            d = d * d
        start_ref[n] = later(s, 1)
        end_ref[n : n + 1, :] = s[SEG - 1 : SEG, :]


def edge_kernel(tokens, rim_ref, head_ref, tap_ref, rate_ref, end_ref, block_ref, change_ref):
    r0, r1 = [[rim_ref[t, j : j + 1, :].astype(f32) for j in range(3)] for t in range(2)]
    h0, h1 = [[head_ref[j, t : t + 1, :].astype(f32) for j in range(3)] for t in range(2)]
    w0, w1, w2 = [[tap_ref[d, j : j + 1, :] for j in range(3)] for d in range(3)]
    more0 = [w1[j] * r1[j] + w2[j] * r0[j] for j in range(3)]
    more1 = [w2[j] * r1[j] for j in range(3)]
    own0 = [w0[j] * h0[j] for j in range(3)]
    own1 = [w0[j] * h1[j] + w1[j] * h0[j] for j in range(3)]
    change0 = (own0[1] + more0[1]) * (own0[2] + more0[2]) - own0[1] * own0[2]
    change1 = (own1[1] + more1[1]) * (own1[2] + more1[2]) - own1[1] * own1[2]
    for i, row in enumerate((change0, change1, more0[0], more1[0])):
        change_ref[i : i + 1, :] = row
    rate = rate_ref[...]
    block_ref[...] = end_ref[...] + jnp.exp(-rate * (tokens - 1.0)) * change0 + jnp.exp(-rate * (tokens - 2.0)) * change1


def local_kernel(query_ref, gated_ref, tap_ref, rate_ref, coef_ref, skip_ref, start_ref, *rest):
    conv_ref, gate_ref, slots = rest[-3:]
    steps = query_ref.shape[0] // SEG
    modes = rate_ref.shape[0]
    queries = Spread(query_ref, slots, steps)
    taps = [rows(tap_ref[d, 0:1, :]) for d in range(3)]
    decay = decays(rate_ref, 1.0)
    coef = [rows(coef_ref[n : n + 1, :]) for n in range(modes)]
    skip = rows(skip_ref[...])
    queries.load_all(steps // CHUNK - 1, 1)
    queries.load_all(0, 0)
    before = (later(queries.at(1, CHUNK - 1), 1), later(queries.at(1, CHUNK - 2), 1))

    def one(k, slot, u, c):
        q1, q2, *state = c
        q0, x = queries.at(slot, u), gated_ref[k]
        gate_ref[k] = taps[0] * q0 + taps[1] * q1 + taps[2] * q2
        state = [d * s + x for d, s in zip(decay, state)]
        conv_ref[k] = total([a * s for a, s in zip(coef, state)] + [skip * x])
        return (q0, q1, *state)

    def ahead(u, b, coming, after):
        if u % 2 == 0:
            queries.load(u // 2, coming, after)

    chunk_loop(steps, one, ahead, (*before, *[start_ref[n] for n in range(modes)]))


def carry_kernel(
    conv_ref, gate_ref, rate_ref, coef_ref, skip_ref, enter_ref, change_ref, out_ref, slots
):
    steps = conv_ref.shape[0]
    modes = rate_ref.shape[0]
    decay = decays(rate_ref, 1.0)
    first = lax.broadcasted_iota(jnp.int32, (SEG, LANES), 0).astype(f32) * steps
    change = [change_ref[0:1, :], change_ref[1:2, :]]
    grow = jnp.exp(rate_ref[...])
    entering = coef_ref[...] * (enter_ref[...] + grow * (change[0] + grow * change[1]))
    part = [jnp.exp(-rate_ref[n : n + 1, :] * first) * entering[n : n + 1, :] for n in range(modes)]

    def one(k, slot, u, part):
        part = [d * s for d, s in zip(decay, part)]
        slots[slot, pl.ds(u, SEG, stride=PITCH), :] = gate_ref[k] * (conv_ref[k] + total(part))
        return part

    def put(seg, chunk, slot):
        start = pl.multiple_of(seg * steps + chunk * CHUNK, CHUNK)
        out_ref[pl.ds(start, CHUNK), :] = slots[slot, pl.ds(seg * PITCH, CHUNK), :]

    def ahead(u, b, coming, after):
        if u % 2 == 0:
            put(u // 2, jnp.maximum(b - 1, 0), after)

    chunk_loop(steps, one, ahead, part)
    chunks = steps // CHUNK
    for seg in range(SEG):
        put(seg, chunks - 1, (chunks - 1) % 2)

    decay = jnp.exp(-rate_ref[...])
    skip = skip_ref[...]
    from0 = jnp.sum(entering * decay - coef_ref[...] * (grow * change[1]), axis=0, keepdims=True)
    from1 = jnp.sum(entering * (decay * decay), axis=0, keepdims=True)
    gate0 = gate_ref[0, 0:1, :] + change_ref[2:3, :]
    gate1 = gate_ref[1, 0:1, :] + change_ref[3:4, :]
    out_ref[0:1, :] = gate0 * (conv_ref[0, 0:1, :] + skip * change[0] + from0)
    out_ref[1:2, :] = gate1 * (conv_ref[1, 0:1, :] + skip * change[1] + from1)


def in_hbm(x):
    return pltpu.with_memory_space_constraint(x, pltpu.HBM)


def windows(groups, rounds):
    counts = [0] * rounds
    order = [*range(1, rounds), 0]
    for i in range(groups):
        counts[order[i % rounds]] += 1
    return counts


def body(streams, short_filter, residues, rates, skip):
    tokens, _, channels = streams.shape
    modes = rates.shape[0]
    steps = tokens // SEG
    groups = channels // LANES
    count, mine = lax.axis_size("seq"), lax.axis_index("seq")
    assert count & (count - 1) == 0 and tokens % (SEG * CHUNK * 2) == 0

    by_stream = in_hbm(jnp.transpose(streams, (1, 0, 2)))
    apart = lax.optimization_barrier(rates)
    coefficient = lax.optimization_barrier(residues * jnp.sqrt(-jnp.expm1(-2.0 * apart)))
    skip = skip[None]

    def stream(j, at):
        return pl.BlockSpec((None, tokens, LANES), lambda c: (j, 0, c + at))

    def cols(*shape, at=0):
        return pl.BlockSpec((*shape, LANES), lambda c: (*[0] * len(shape), c + at))

    segs_shape = pltpu.HBM((steps, SEG, channels), f32)
    slots = pltpu.VMEM((2, SEG * PITCH, LANES), f32)
    anywhere = pl.BlockSpec(memory_space=pl.ANY)
    params = pltpu.CompilerParams(vmem_limit_bytes=VMEM_LIMIT)

    rim = lax.ppermute(streams[tokens - 2 :], "seq", [(i, i + 1) for i in range(count - 1)])

    gated, starts, end = pl.pallas_call(
        states_kernel,
        grid=(groups,),
        in_specs=[stream(1, 0), stream(2, 0), cols(3, 3), cols(modes)],
        out_specs=[cols(steps, SEG), cols(modes, SEG), cols(modes)],
        out_shape=[
            segs_shape,
            jax.ShapeDtypeStruct((modes, SEG, channels), f32),
            jax.ShapeDtypeStruct((modes, channels), f32),
        ],
        scratch_shapes=[slots, slots],
        compiler_params=params,
        name="states",
    )(by_stream, by_stream, short_filter, rates)

    end, change = pl.pallas_call(
        functools.partial(edge_kernel, tokens),
        grid=(1,),
        in_specs=[
            pl.BlockSpec((2, 3, channels), lambda i: (0, 0, 0)),
            pl.BlockSpec((3, CHUNK, channels), lambda i: (0, 0, 0)),
            pl.BlockSpec((3, 3, channels), lambda i: (0, 0, 0)),
            pl.BlockSpec((modes, channels), lambda i: (0, 0)),
            pl.BlockSpec((modes, channels), lambda i: (0, 0)),
        ],
        out_specs=[pl.BlockSpec((modes, channels), lambda i: (0, 0)), pl.BlockSpec((4, channels), lambda i: (0, 0))],
        out_shape=[jax.ShapeDtypeStruct((modes, channels), f32), jax.ShapeDtypeStruct((4, channels), f32)],
        compiler_params=params,
        name="edge",
    )(rim, by_stream, short_filter, rates, end)

    rounds = count.bit_length() - 1
    block, entering = end, jnp.zeros_like(end)
    made, at = (), 0
    for r, beside in enumerate(windows(groups, rounds)):
        size = 1 << r
        other = lax.ppermute(block, "seq", [(i, i ^ size) for i in range(count)])
        if beside:
            inputs = [by_stream, in_hbm(gated), short_filter, rates, coefficient, skip, starts]
            made = pl.pallas_call(
                local_kernel,
                grid=(beside,),
                in_specs=[
                    stream(0, at),
                    cols(steps, SEG, at=at),
                    cols(3, 3, at=at),
                    cols(modes, at=at),
                    cols(modes, at=at),
                    cols(1, at=at),
                    cols(modes, SEG, at=at),
                    *[anywhere] * len(made),
                ],
                out_specs=[cols(steps, SEG, at=at)] * 2,
                out_shape=[segs_shape, segs_shape],
                input_output_aliases={len(inputs) + i: i for i in range(len(made))},
                scratch_shapes=[slots],
                compiler_params=params,
        name="local",
            )(*inputs, *made)
            at += beside
        second = (mine & size) != 0
        behind = (mine & (size - 1)).astype(f32) * tokens
        entering = jnp.where(second, entering + jnp.exp(-rates * behind) * other, entering)
        across = jnp.exp(-rates * float(tokens * size))
        block = jnp.where(second, block + across * other, other + across * block)
    conv, gate = made

    return pl.pallas_call(
        carry_kernel,
        grid=(groups,),
        in_specs=[
            cols(steps, SEG),
            cols(steps, SEG),
            cols(modes),
            cols(modes),
            cols(1),
            cols(modes),
            cols(4),
        ],
        out_specs=cols(tokens),
        out_shape=pltpu.HBM((tokens, channels), f32),
        scratch_shapes=[slots],
        compiler_params=params,
        name="carry",
    )(in_hbm(conv), in_hbm(gate), rates, coefficient, skip, entering, change)


def solution(mesh):
    placed = (P(("groups", "seq"), None, None), P(), P(), P(), P())

    return jax.shard_map(
        body, mesh=mesh, in_specs=placed, out_specs=P(("groups", "seq"), None), check_vma=False
    )
```

time: 63.3 us -> 63.4 us (level)
  Pallas kernels: 37.1 us -> 42.4 us
  starting transfers between devices: 13.6 us -> 11 us
  waiting for transfers between devices: 8.83 us -> 6.43 us
  other arithmetic: 2.29 us -> 0.19 us
  local copies, waits for them, and re-layouts: 0.82 us -> 2.47 us
    pallas_call x3 -> x7, Pallas kernels: 37.1 us -> 42.4 us  [the longest x4 21 us: body(): pl.pallas_call(local_kernel, grid=(beside,), in_specs=[stream(0, at), col...]
    ppermute x4, starting transfers between devices: 11.2 us -> 8.57 us  [body(): other = lax.ppermute(block, 'seq', [(i, i ^ size) for i in range(count)])]
    unnamed x4 -> x13, local copies, waits for them, and re-layouts: 0.01 us -> 1.66 us
    ppermute x4, waiting for transfers between devices: 8.02 us -> 6.42 us  [body(): other = lax.ppermute(block, 'seq', [(i, i ^ size) for i in range(count)])]
    select_n x3, other arithmetic: 0.92 us -> 0.08 us  [body(): block = jnp.where(second, block + across * other, other + across * block)]
    ppermute x1, waiting for transfers between devices: 0.82 us -> 0.01 us  [body(): lax.ppermute(streams[tokens - 2:], 'seq', [(i, i + 1) for i in range(coun...]
    mul x1, other arithmetic: 0.76 us -> 0.05 us  [body(): residues * jnp.sqrt(-jnp.expm1(-2.0 * apart))]
  transfers between devices with their start and end apart: 5 -> 5, of which waited for: 5 -> 3; matrix products, arithmetic and copies ran while one was open for 0% -> 0% of each run, Pallas kernels for 0% -> 50%
where the time goes in v2:
time: 63.4 us; the launch traced here: 62.6 us
  Pallas kernels  42.4 us (67%)
  starting transfers between devices  11 us (17%)
  waiting for transfers between devices  6.43 us (10%)
  local copies, waits for them, and re-layouts  2.47 us (4%)
    pallas_call x4, Pallas kernels, body(): pl.pallas_call(local_kernel, grid=(beside,), in_specs=[stream(0, at), col...  21 us
    pallas_call x1, Pallas kernels, body(): pl.pallas_call(states_kernel, grid=(groups,), in_specs=[stream(1, 0), str...  10.5 us
    pallas_call x1, Pallas kernels, body(): pl.pallas_call(carry_kernel, grid=(groups,), in_specs=[cols(steps, SEG),...  9.85 us
    ppermute x4, starting transfers between devices, body(): other = lax.ppermute(block, 'seq', [(i, i ^ size) for i in range(count)])  8.57 us
    ppermute x4, waiting for transfers between devices, body(): other = lax.ppermute(block, 'seq', [(i, i ^ size) for i in range(count)])  6.42 us
    ppermute x1, starting transfers between devices, body(): lax.ppermute(streams[tokens - 2:], 'seq', [(i, i + 1) for i in range(coun...  2.4 us
    unnamed x13, local copies, waits for them, and re-layouts  1.66 us
  transfers between devices with their start and end apart: 5, of which 3 were waited for; matrix products, arithmetic and copies ran while one was open for 0% of the time, Pallas kernels for 50%

profile of v2, /device:TPU:0, one launch (start us, length us, event | category | flops | bytes accessed | tf_op | source)
XLA Modules:
  0.0 62.6 jit_solution(16419248417605472654)
XLA Ops:
  0.0 0.8 %slice.3 = bf16[2,3,1024]{2,0,1:T(2,128)(2,1)S(1)} slice(bf16[1024,3,1024]{2,0,1:T(8,128)(2,1)} %param.5), slice={[1022:1024], [0:3], [0:1024]} | slice | bytes 24576 | tf_op jit(solution)/shard_map/slice | solution.py:225
  0.8 2.4 %collective-permute-start = (bf16[2,3,1024]{2,1,0:T(4,128)(2,1)S(1)}, bf16[2,3,1024]{2,1,0:T(4,128)(2,1)S(1)}, u32[]{:S(2)}, u32[]{:S(2)}) collective-permute-start(bf16[2,3,1024]{2,1,0:T(4,128)(2,1)S(1)} %copy.13), channel_id=1, source_target_pairs={{0,1},{1,2},{2,3},{3,4},{4,5},{5,6},{6,7},{7,8},{8,9},{9,10},{10,1... | collective-permute-start | bytes 36872 | tf_op jit(solution)/shard_map/ppermute | solution.py:225
  3.2 0.0 copy-start
  3.2 0.8 %copy-done = f32[16,1024]{1,0:T(8,128)S(1)} copy-done((f32[16,1024]{1,0:T(8,128)S(1)}, f32[16,1024]{1,0:T(8,128)}, u32[]{:S(2)}) %copy-start) | copy-done | bytes 65560
  4.1 0.8 %copy-done.2 = f32[3,3,1024]{2,1,0:T(4,128)S(1)} copy-done((f32[3,3,1024]{2,1,0:T(4,128)S(1)}, f32[3,3,1024]{2,1,0:T(4,128)}, u32[]{:S(2)}) %copy-start.2) | copy-done | bytes 36888
  4.9 10.5 %states.1 = (f32[128,8,1024]{2,1,0:T(8,128)}, f32[16,8,1024]{2,1,0:T(8,128)S(1)}, f32[16,1024]{1,0:T(8,128)S(1)}) custom-call(bf16[3,1024,1024]{2,1,0:T(8,128)(2,1)} %bitcast.7, bf16[3,1024,1024]{2,1,0:T(8,128)(2,1)} %bitcast.8, f32[3,3,1024]{2,1,0:T(4,128)S(1)} %copy-done.2, f32[16,1024]{1,0:T(8,128)S(1)} %copy-done), custom_call_target="tpu_custom_call" | custom-call | tf_op jit(solution)/shard_map/states/pallas_call | solution.py:227
  15.4 0.0 copy-start.4
  15.4 0.0 collective-permute-done.rim_ref
  15.4 1.0 %edge.1 = (f32[16,1024]{1,0:T(8,128)S(1)}, f32[4,1024]{1,0:T(4,128)S(1)}) custom-call(bf16[2,3,1024]{2,1,0:T(4,128)(2,1)S(1)} %collective-permute-done.rim_ref, bf16[3,1024,1024]{2,1,0:T(8,128)(2,1)} %bitcast.9, f32[3,3,1024]{2,1,0:T(4,128)S(1)} %copy-done.2, f32[16,1024]{1,0:T(8,128)S(1)} %copy-done, f32[16,1024]{1,0:T(8,128)S(1)} %get-tuple-element.28.end_ref), custom_call_target="tpu_custom_call" | custom-call | tf_op jit(solution)/shard_map/edge/pallas_call | solution.py:242
  16.5 2.7 %collective-permute-start.1 = (f32[16,1024]{1,0:T(8,128)S(1)}, f32[16,1024]{1,0:T(8,128)S(1)}, u32[]{:S(2)}, u32[]{:S(2)}) collective-permute-start(f32[16,1024]{1,0:T(8,128)S(1)} %get-tuple-element.29), channel_id=1, source_target_pairs={{0,1},{1,0},{2,3},{3,2},{4,5},{5,4},{6,7},{7,6},{8,9},{9,8},{10,11... | collective-permute-start | bytes 196616 | tf_op jit(solution)/shard_map/ppermute | solution.py:263
  19.1 0.9 %collective-permute-done.1 = f32[16,1024]{1,0:T(8,128)S(1)} collective-permute-done((f32[16,1024]{1,0:T(8,128)S(1)}, f32[16,1024]{1,0:T(8,128)S(1)}, u32[]{:S(2)}, u32[]{:S(2)}) %collective-permute-start.1) | collective-permute-done | bytes 65568 | tf_op jit(solution)/shard_map/ppermute | solution.py:263
  20.0 0.0 copy-done.1
  20.1 1.6 %collective-permute-start.2 = (f32[16,1024]{1,0:T(8,128)S(1)}, f32[16,1024]{1,0:T(8,128)S(1)}, u32[]{:S(2)}, u32[]{:S(2)}) collective-permute-start(f32[16,1024]{1,0:T(8,128)S(1)} %add_select_fusion.5), channel_id=1, source_target_pairs={{0,2},{1,3},{2,0},{3,1},{4,6},{5,7},{6,4},{7,5},{8,10},{9,11},{10,... | collective-permute-start | bytes 196616 | tf_op jit(solution)/shard_map/ppermute | solution.py:263
  21.7 2.8 %collective-permute-done.2 = f32[16,1024]{1,0:T(8,128)S(1)} collective-permute-done((f32[16,1024]{1,0:T(8,128)S(1)}, f32[16,1024]{1,0:T(8,128)S(1)}, u32[]{:S(2)}, u32[]{:S(2)}) %collective-permute-start.2) | collective-permute-done | bytes 65568 | tf_op jit(solution)/shard_map/ppermute | solution.py:263
  24.5 1.6 %collective-permute-start.3 = (f32[16,1024]{1,0:T(8,128)S(1)}, f32[16,1024]{1,0:T(8,128)S(1)}, u32[]{:S(2)}, u32[]{:S(2)}) collective-permute-start(f32[16,1024]{1,0:T(8,128)S(1)} %add_select_fusion.4), channel_id=1, source_target_pairs={{0,4},{1,5},{2,6},{3,7},{4,0},{5,1},{6,2},{7,3},{8,12},{9,13},{10,... | collective-permute-start | bytes 196616 | tf_op jit(solution)/shard_map/ppermute | solution.py:263
  26.2 2.7 %collective-permute-done.3 = f32[16,1024]{1,0:T(8,128)S(1)} collective-permute-done((f32[16,1024]{1,0:T(8,128)S(1)}, f32[16,1024]{1,0:T(8,128)S(1)}, u32[]{:S(2)}, u32[]{:S(2)}) %collective-permute-start.3) | collective-permute-done | bytes 65568 | tf_op jit(solution)/shard_map/ppermute | solution.py:263
  28.9 2.7 %collective-permute-start.4 = (f32[16,1024]{1,0:T(8,128)S(1)}, f32[16,1024]{1,0:T(8,128)S(1)}, u32[]{:S(2)}, u32[]{:S(2)}) collective-permute-start(f32[16,1024]{1,0:T(8,128)S(1)} %add_select_fusion.3), channel_id=1, source_target_pairs={{0,8},{1,9},{2,10},{3,11},{4,12},{5,13},{6,14},{7,15},{8,0},{9,1},... | collective-permute-start | bytes 196616 | tf_op jit(solution)/shard_map/ppermute | solution.py:263
  31.6 5.3 %local.4 = (f32[128,8,1024]{2,1,0:T(8,128)}, f32[128,8,1024]{2,1,0:T(8,128)}) custom-call(bf16[3,1024,1024]{2,1,0:T(8,128)(2,1)} %bitcast.10, f32[128,8,1024]{2,1,0:T(8,128)} %get-tuple-element.18.gated_ref, f32[3,3,1024]{2,1,0:T(4,128)S(1)} %copy-done.3, f32[16,1024]{1,0:T(8,128)S(1)} %copy-done.1, f32[16,1024]{1,0:T(8,128)S(1)} %sqrt_multiply_fusion.coef_ref, ...), custom_call_target="tpu_custom_call" | custom-call | tf_op jit(solution)/shard_map/local/pallas_call | solution.py:266
  36.9 5.3 %local.5 = (f32[128,8,1024]{2,1,0:T(8,128)}, f32[128,8,1024]{2,1,0:T(8,128)}) custom-call(bf16[3,1024,1024]{2,1,0:T(8,128)(2,1)} %bitcast.11, f32[128,8,1024]{2,1,0:T(8,128)} %get-tuple-element.18.gated_ref, f32[3,3,1024]{2,1,0:T(4,128)S(1)} %copy-done.3, f32[16,1024]{1,0:T(8,128)S(1)} %copy-done.1, ...), custom_call_target="tpu_custom_call", output_to_operand_aliasing={{0}: (7, {}), {1}: (8, {})} | custom-call | tf_op jit(solution)/shard_map/local/pallas_call | solution.py:266
  42.1 5.3 %local.6 = (f32[128,8,1024]{2,1,0:T(8,128)}, f32[128,8,1024]{2,1,0:T(8,128)}) custom-call(bf16[3,1024,1024]{2,1,0:T(8,128)(2,1)} %bitcast.12, f32[128,8,1024]{2,1,0:T(8,128)} %get-tuple-element.18.gated_ref, f32[3,3,1024]{2,1,0:T(4,128)S(1)} %copy-done.3, f32[16,1024]{1,0:T(8,128)S(1)} %copy-done.1, ...), custom_call_target="tpu_custom_call", output_to_operand_aliasing={{0}: (7, {}), {1}: (8, {})} | custom-call | tf_op jit(solution)/shard_map/local/pallas_call | solution.py:266
  47.4 5.3 %local.7 = (f32[128,8,1024]{2,1,0:T(8,128)}, f32[128,8,1024]{2,1,0:T(8,128)}) custom-call(bf16[3,1024,1024]{2,1,0:T(8,128)(2,1)} %bitcast.13, f32[128,8,1024]{2,1,0:T(8,128)} %get-tuple-element.18.gated_ref, f32[3,3,1024]{2,1,0:T(4,128)S(1)} %copy-done.3, f32[16,1024]{1,0:T(8,128)S(1)} %copy-done.1, ...), custom_call_target="tpu_custom_call", output_to_operand_aliasing={{0}: (7, {}), {1}: (8, {})} | custom-call | tf_op jit(solution)/shard_map/local/pallas_call | solution.py:266
  52.6 0.0 collective-permute-done.4
  52.7 0.1 add_select_fusion.enter_ref
  52.7 9.9 %carry.1 = f32[1024,1024]{1,0:T(8,128)} custom-call(f32[128,8,1024]{2,1,0:T(8,128)} %get-tuple-element.26.conv_ref, f32[128,8,1024]{2,1,0:T(8,128)} %get-tuple-element.27.gate_ref, f32[16,1024]{1,0:T(8,128)S(1)} %copy-done.1, f32[16,1024]{1,0:T(8,128)S(1)} %sqrt_multiply_fusion.coef_ref, f32[1,1024]{1,0:T(1,128)S(1)} %bitcast.6, ...), custom_call_target="tpu_custom_call" | custom-call | tf_op jit(solution)/shard_map/carry/pallas_call | solution.py:294
  (12 shorter events, 0.1 us)
Async XLA Ops:
  0.8 14.6 %collective-permute-start = (bf16[2,3,1024]{2,1,0:T(4,128)(2,1)S(1)}, bf16[2,3,1024]{2,1,0:T(4,128)(2,1)S(1)}, u32[]{:S(2)}, u32[]{:S(2)}) collective-permute-start(bf16[2,3,1024]{2,1,0:T(4,128)(2,1)S(1)} %copy.13), channel_id=1, source_target_pairs={{0,1},{1,2},{2,3},{3,4},{4,5},{5,6},{6,7},{7,8},{8,9},{9,10},{10,1... | collective-permute-start | bytes 36872 | tf_op jit(solution)/shard_map/ppermute | solution.py:225
  3.2 0.8 %copy-start = (f32[16,1024]{1,0:T(8,128)S(1)}, f32[16,1024]{1,0:T(8,128)}, u32[]{:S(2)}) copy-start(f32[16,1024]{1,0:T(8,128)} %rate_ref.13) | copy-start | bytes 196612
  4.1 0.8 %copy-start.2 = (f32[3,3,1024]{2,1,0:T(4,128)S(1)}, f32[3,3,1024]{2,1,0:T(4,128)}, u32[]{:S(2)}) copy-start(f32[3,3,1024]{2,1,0:T(4,128)} %tap_ref.11) | copy-start | bytes 110596
  15.4 4.6 %copy-start.1 = (f32[16,1024]{1,0:T(8,128)S(1)}, f32[16,1024]{1,0:T(8,128)}, u32[]{:S(2)}) copy-start(f32[16,1024]{1,0:T(8,128)} %rate_ref.13) | copy-start | bytes 196612
  15.4 16.1 %copy-start.5 = (f32[16,1024]{1,0:T(8,128)S(1)}, f32[16,1024]{1,0:T(8,128)}, u32[]{:S(2)}) copy-start(f32[16,1024]{1,0:T(8,128)} %param.7) | copy-start | bytes 196612
  15.4 16.2 %copy-start.3 = (f32[3,3,1024]{2,1,0:T(4,128)S(1)}, f32[3,3,1024]{2,1,0:T(4,128)}, u32[]{:S(2)}) copy-start(f32[3,3,1024]{2,1,0:T(4,128)} %tap_ref.11) | copy-start | bytes 110596
  15.4 16.2 %copy-start.4 = (f32[1024]{0:T(1024)S(1)}, f32[1024]{0:T(1024)}, u32[]{:S(2)}) copy-start(f32[1024]{0:T(1024)} %param.9) | copy-start | bytes 12292
  16.5 3.6 %collective-permute-start.1 = (f32[16,1024]{1,0:T(8,128)S(1)}, f32[16,1024]{1,0:T(8,128)S(1)}, u32[]{:S(2)}, u32[]{:S(2)}) collective-permute-start(f32[16,1024]{1,0:T(8,128)S(1)} %get-tuple-element.29), channel_id=1, source_target_pairs={{0,1},{1,0},{2,3},{3,2},{4,5},{5,4},{6,7},{7,6},{8,9},{9,8},{10,11... | collective-permute-start | bytes 196616 | tf_op jit(solution)/shard_map/ppermute | solution.py:263
  20.1 4.4 %collective-permute-start.2 = (f32[16,1024]{1,0:T(8,128)S(1)}, f32[16,1024]{1,0:T(8,128)S(1)}, u32[]{:S(2)}, u32[]{:S(2)}) collective-permute-start(f32[16,1024]{1,0:T(8,128)S(1)} %add_select_fusion.5), channel_id=1, source_target_pairs={{0,2},{1,3},{2,0},{3,1},{4,6},{5,7},{6,4},{7,5},{8,10},{9,11},{10,... | collective-permute-start | bytes 196616 | tf_op jit(solution)/shard_map/ppermute | solution.py:263
  24.5 4.3 %collective-permute-start.3 = (f32[16,1024]{1,0:T(8,128)S(1)}, f32[16,1024]{1,0:T(8,128)S(1)}, u32[]{:S(2)}, u32[]{:S(2)}) collective-permute-start(f32[16,1024]{1,0:T(8,128)S(1)} %add_select_fusion.4), channel_id=1, source_target_pairs={{0,4},{1,5},{2,6},{3,7},{4,0},{5,1},{6,2},{7,3},{8,12},{9,13},{10,... | collective-permute-start | bytes 196616 | tf_op jit(solution)/shard_map/ppermute | solution.py:263
  28.9 23.8 %collective-permute-start.4 = (f32[16,1024]{1,0:T(8,128)S(1)}, f32[16,1024]{1,0:T(8,128)S(1)}, u32[]{:S(2)}, u32[]{:S(2)}) collective-permute-start(f32[16,1024]{1,0:T(8,128)S(1)} %add_select_fusion.3), channel_id=1, source_target_pairs={{0,8},{1,9},{2,10},{3,11},{4,12},{5,13},{6,14},{7,15},{8,0},{9,1},... | collective-permute-start | bytes 196616 | tf_op jit(solution)/shard_map/ppermute | solution.py:263

commit v3 on v0

v3 whole, which is shorter than its diff:
```python
import functools

import jax
import jax.numpy as jnp
from jax import lax
from jax.experimental import pallas as pl
from jax.experimental.pallas import tpu as pltpu
from jax.sharding import PartitionSpec as P


SEG = 8
LANES = 128
CHUNK = 16
PITCH = CHUNK + 8
EDGE = 16
VMEM_LIMIT = 16 << 20
f32 = jnp.float32


def rows(vec):
    return jnp.broadcast_to(vec, (SEG, LANES))


def total(parts):
    while len(parts) > 1:
        tail = [parts[-1]] if len(parts) % 2 else []
        parts = [a + b for a, b in zip(parts[::2], parts[1::2])] + tail
    return parts[0]


def later(x, by):
    row = lax.broadcasted_iota(jnp.int32, x.shape, 0)
    return jnp.where(row >= by, pltpu.roll(x, by, 0), 0.0)


def each(ref, at):
    return [rows(ref[n : n + 1, at]) for n in range(ref.shape[0])]


class Spread:
    def __init__(self, block, slots, steps):
        self.block, self.slots, self.steps = block, slots, steps

    def load(self, seg, chunk, slot):
        start = pl.multiple_of(seg * self.steps + chunk * CHUNK, CHUNK)
        piece = self.block[pl.ds(start, CHUNK), :].astype(f32)
        self.slots[slot, pl.ds(seg, CHUNK, stride=SEG), :] = piece

    def load_all(self, chunk, slot):
        for seg in range(SEG):
            self.load(seg, chunk, slot)

    def at(self, slot, k):
        return self.slots[slot, pl.ds(k * SEG, SEG), :]


def chunk_loop(steps, one, ahead, start):
    chunks = steps // CHUNK

    def trip(b, c):
        slot, after = lax.rem(b, 2), lax.rem(b + 1, 2)
        coming = lax.rem(b + 1, chunks)
        for u in range(CHUNK):
            c = one(b * CHUNK + u, slot, u, c)
            ahead(u, b, coming, after)
        return c

    return lax.fori_loop(0, chunks, trip, start)


def lanes(c):
    return pl.ds(pl.multiple_of(c * LANES, LANES), LANES)


def states_kernel(
    stream_ref, tap_ref, rate_ref,
    gated_ref, start_ref, send_ref, query_ref, taps_ref, rates_ref, decay_ref, enter_ref,
    raw, head, stride_decay, key_slots, val_slots, raw_sem, query_sem, small_sem,
):
    groups, steps = gated_ref.shape[:2]
    modes, tokens = rate_ref.shape[0], steps * SEG

    def fetch(c, slot):
        return pltpu.make_async_copy(stream_ref.at[1:3, :, lanes(c)], raw.at[slot], raw_sem.at[slot])

    def fetch_query(c):
        return pltpu.make_async_copy(stream_ref.at[0, :, lanes(c)], query_ref.at[c], query_sem.at[c])

    small = [
        pltpu.make_async_copy(rate_ref, rates_ref, small_sem.at[0]),
        pltpu.make_async_copy(tap_ref, taps_ref, small_sem.at[1]),
        pltpu.make_async_copy(stream_ref.at[:, 0:CHUNK, :], head.at[0], small_sem.at[2]),
        pltpu.make_async_copy(stream_ref.at[:, pl.ds(tokens - CHUNK, CHUNK), :], head.at[1], small_sem.at[3]),
    ]
    fetch(0, 0).start()
    for copy in small:
        copy.start()
    for copy in small:
        copy.wait()
    decay_ref[...] = jnp.exp(-rates_ref[...])
    stride_decay[...] = jnp.exp(-rates_ref[...] * float(steps))
    enter_ref[...] = jnp.zeros_like(enter_ref)
    edge = [head[1, j, CHUNK - 2 :, :].astype(f32) for j in (1, 2, 0)] + [head[0, j, :2, :].astype(f32) for j in (1, 2)]
    for i, pair in enumerate(edge):
        send_ref[modes + 2 * i : modes + 2 * i + 2, :] = pair
    send_ref[modes + 2 * len(edge) :, :] = jnp.zeros((EDGE - 2 * len(edge), send_ref.shape[1]), f32)

    def group(c, _):
        slot = lax.rem(c, 2)

        @pl.when(c + 1 < groups)
        def _():
            fetch(c + 1, 1 - slot).start()

        fetch_query(c).start()
        fetch(c, slot).wait()
        keys = Spread(raw.at[slot, 0], key_slots, steps)
        vals = Spread(raw.at[slot, 1], val_slots, steps)
        at = lanes(c)
        taps = [[rows(taps_ref[d, j : j + 1, at]) for d in range(3)] for j in (1, 2)]
        decay = each(decay_ref, at)
        before = []
        for part in (keys, vals):
            part.load_all(steps // CHUNK - 1, 1)
            part.load_all(0, 0)
            before += [later(part.at(1, CHUNK - 1), 1), later(part.at(1, CHUNK - 2), 1)]

        def one(k, slot, u, carried):
            k1, k2, v1, v2, *state = carried
            k0, v0 = keys.at(slot, u), vals.at(slot, u)
            a = taps[0][0] * k0 + taps[0][1] * k1 + taps[0][2] * k2
            b = taps[1][0] * v0 + taps[1][1] * v1 + taps[1][2] * v2
            x = a * b
            gated_ref[c, k] = x
            return (k0, k1, v0, v1, *[d * s + x for d, s in zip(decay, state)])

        def ahead(u, b, coming, after):
            (keys, vals)[u % 2].load(u // 2, coming, after)

        zero = jnp.zeros((SEG, LANES), f32)
        final = chunk_loop(steps, one, ahead, (*before, *[zero] * modes))[4:]
        for n, d in enumerate(each(stride_decay, at)):
            s = final[n]
            for by in (1, 2, 4):
                s = s + d * later(s, by)
                d = d * d
            start_ref[c, n] = later(s, 1)
            send_ref[n : n + 1, at] = s[SEG - 1 : SEG, :]
        return 0

    lax.fori_loop(0, groups, group, 0)

    def landed(c, _):
        fetch_query(c).wait()
        return 0

    lax.fori_loop(0, groups, landed, 0)


def join_kernel(size, tokens, tap_ref, rate_ref, other_ref, mine_ref, enter_ref, enter_out, *mine_out):
    modes = rate_ref.shape[0]
    place = lax.axis_index("seq")
    second = (place & size) != 0
    rate = rate_ref[...]

    def after(times):
        return jnp.exp(-rate * times)

    def change(early, late):
        rim = [early[modes + i : modes + i + 1, :] for i in range(6)]
        head = [late[modes + i : modes + i + 1, :] for i in range(6, 10)]
        w = [[tap_ref[d, j : j + 1, :] for d in range(3)] for j in (1, 2, 0)]
        more0 = [w[j][1] * rim[2 * j + 1] + w[j][2] * rim[2 * j] for j in range(3)]
        more1 = [w[j][2] * rim[2 * j + 1] for j in range(3)]
        own0 = [w[j][0] * head[2 * j] for j in range(2)]
        own1 = [w[j][0] * head[2 * j + 1] + w[j][1] * head[2 * j] for j in range(2)]
        change0 = (own0[0] + more0[0]) * (own0[1] + more0[1]) - own0[0] * own0[1]
        change1 = (own1[0] + more1[0]) * (own1[1] + more1[1]) - own1[0] * own1[1]
        return change0, change1, more0[2], more1[2]

    def merge(early, late, out, change0, change1):
        span = float(tokens * size)
        out[:modes, :] = (
            late[:modes, :] + after(span) * early[:modes, :] + after(span - 1.0) * change0 + after(span - 2.0) * change1
        )
        out[modes : modes + 6, :] = late[modes : modes + 6, :]
        out[modes + 6 :, :] = early[modes + 6 :, :]

    @pl.when(second)
    def _():
        edge = change(other_ref, mine_ref)
        before = place & (size - 1)
        span = before.astype(f32) * float(tokens)
        enter_out[:modes, :] = (
            enter_ref[:modes, :]
            + after(span) * other_ref[:modes, :]
            + after(span - 1.0) * edge[0]
            + after(span - 2.0) * edge[1]
        )
        enter_out[modes:, :] = enter_ref[modes:, :]

        @pl.when(before == 0)
        def _():
            for i, row in enumerate(edge):
                enter_out[modes + i : modes + i + 1, :] = row

        if mine_out:
            merge(other_ref, mine_ref, mine_out[0], *edge[:2])

    @pl.when(jnp.logical_not(second))
    def _():
        enter_out[...] = enter_ref[...]
        if mine_out:
            merge(mine_ref, other_ref, mine_out[0], *change(mine_ref, other_ref)[:2])


def local_kernel(at, beside, query_ref, gated_ref, tap_ref, decay_ref, coef_ref, skip_ref, start_ref, *rest):
    conv_ref, gate_ref, slots = rest[-3:]
    steps = gated_ref.shape[1]
    modes = decay_ref.shape[0]

    def group(i, _):
        c = i + at
        on = lanes(c)
        queries = Spread(query_ref.at[c], slots, steps)
        taps = [rows(tap_ref[d, 0:1, on]) for d in range(3)]
        decay, coef = each(decay_ref, on), each(coef_ref, on)
        skip = rows(skip_ref[:, on])
        queries.load_all(steps // CHUNK - 1, 1)
        queries.load_all(0, 0)
        before = (later(queries.at(1, CHUNK - 1), 1), later(queries.at(1, CHUNK - 2), 1))

        def one(k, slot, u, carried):
            q1, q2, *state = carried
            q0, x = queries.at(slot, u), gated_ref[c, k]
            gate_ref[c, k] = taps[0] * q0 + taps[1] * q1 + taps[2] * q2
            state = [d * s + x for d, s in zip(decay, state)]
            conv_ref[c, k] = total([a * s for a, s in zip(coef, state)] + [skip * x])
            return (q0, q1, *state)

        def ahead(u, b, coming, after):
            if u % 2 == 0:
                queries.load(u // 2, coming, after)

        chunk_loop(steps, one, ahead, (*before, *[start_ref[c, n] for n in range(modes)]))
        return 0

    lax.fori_loop(0, beside, group, 0)


def carry_kernel(conv_ref, gate_ref, rate_ref, decay_ref, coef_ref, skip_ref, enter_ref, out_ref, mixed, slots, sem):
    groups, steps = conv_ref.shape[:2]
    modes, chunks = rate_ref.shape[0], steps // CHUNK

    def store(c, side):
        return pltpu.make_async_copy(mixed.at[side], out_ref.at[:, lanes(c)], sem.at[side])

    def group(c, _):
        side, on = lax.rem(c, 2), lanes(c)

        @pl.when(c >= 2)
        def _():
            store(c - 2, side).wait()

        rate, weight = rate_ref[:, on], coef_ref[:, on]
        decay = each(decay_ref, on)
        first = lax.broadcasted_iota(jnp.int32, (SEG, LANES), 0).astype(f32) * steps
        entering = weight * enter_ref[:modes, on]
        part = [jnp.exp(-rate[n : n + 1, :] * first) * entering[n : n + 1, :] for n in range(modes)]

        def one(k, slot, u, part):
            part = [d * s for d, s in zip(decay, part)]
            slots[slot, pl.ds(u, SEG, stride=PITCH), :] = gate_ref[c, k] * (conv_ref[c, k] + total(part))
            return part

        def put(seg, chunk, slot):
            start = pl.multiple_of(seg * steps + chunk * CHUNK, CHUNK)
            mixed[side, pl.ds(start, CHUNK), :] = slots[slot, pl.ds(seg * PITCH, CHUNK), :]

        def ahead(u, b, coming, after):
            if u % 2 == 0:
                put(u // 2, jnp.maximum(b - 1, 0), after)

        chunk_loop(steps, one, ahead, part)
        for seg in range(SEG):
            put(seg, chunks - 1, (chunks - 1) % 2)

        once = decay_ref[:, on]
        skip = skip_ref[:, on]
        change = [enter_ref[modes + i : modes + i + 1, on] for i in range(4)]
        from0 = jnp.sum(entering * once - weight * (jnp.exp(rate) * change[1]), axis=0, keepdims=True)
        from1 = jnp.sum(entering * (once * once), axis=0, keepdims=True)
        gate0 = gate_ref[c, 0, 0:1, :] + change[2]
        gate1 = gate_ref[c, 1, 0:1, :] + change[3]
        mixed[side, 0:1, :] = gate0 * (conv_ref[c, 0, 0:1, :] + skip * change[0] + from0)
        mixed[side, 1:2, :] = gate1 * (conv_ref[c, 1, 0:1, :] + skip * change[1] + from1)
        store(c, side).start()
        return 0

    lax.fori_loop(0, groups, group, 0)
    for c in range(max(groups - 2, 0), groups):
        store(c, c % 2).wait()


def in_hbm(x):
    return pltpu.with_memory_space_constraint(x, pltpu.HBM)


def windows(groups, rounds):
    counts = [0] * rounds
    order = [*range(1, rounds), 0]
    for i in range(groups):
        counts[order[i % rounds] if i < rounds else 1 + (i - rounds) % (rounds - 1)] += 1
    return counts


def body(streams, short_filter, residues, rates, skip):
    tokens, _, channels = streams.shape
    modes = rates.shape[0]
    steps = tokens // SEG
    groups = channels // LANES
    count = lax.axis_size("seq")
    assert count & (count - 1) == 0 and tokens % (SEG * CHUNK * 2) == 0

    by_stream = in_hbm(jnp.transpose(streams, (1, 0, 2)))
    apart = lax.optimization_barrier(rates)
    coefficient = lax.optimization_barrier(residues * jnp.sqrt(-jnp.expm1(-2.0 * apart)))
    skip = skip[None]

    segs = pltpu.VMEM((groups, steps, SEG, LANES), f32)
    spread = pltpu.VMEM((2, SEG * CHUNK, LANES), f32)
    slots = pltpu.VMEM((2, SEG * PITCH, LANES), f32)
    hbm = pl.BlockSpec(memory_space=pltpu.HBM)
    whole = pl.BlockSpec(memory_space=pltpu.VMEM)
    params = pltpu.CompilerParams(vmem_limit_bytes=VMEM_LIMIT)

    block_shape = pltpu.VMEM((modes + EDGE, channels), f32)
    enter_shape = pltpu.VMEM((modes + 4, channels), f32)
    mode_shape = pltpu.VMEM((modes, channels), f32)

    gated, starts, block, query, taps, rate, decay, entering = pl.pallas_call(
        states_kernel,
        in_specs=[hbm] * 3,
        out_specs=[whole] * 8,
        out_shape=[
            segs,
            pltpu.VMEM((groups, modes, SEG, LANES), f32),
            block_shape,
            pltpu.VMEM((groups, tokens, LANES), streams.dtype),
            pltpu.VMEM(short_filter.shape, f32),
            mode_shape,
            mode_shape,
            enter_shape,
        ],
        scratch_shapes=[
            pltpu.VMEM((2, 2, tokens, LANES), streams.dtype),
            pltpu.VMEM((2, 3, CHUNK, channels), streams.dtype),
            mode_shape,
            spread,
            spread,
            pltpu.SemaphoreType.DMA((2,)),
            pltpu.SemaphoreType.DMA((groups,)),
            pltpu.SemaphoreType.DMA((4,)),
        ],
        compiler_params=params,
        name="states",
    )(by_stream, in_hbm(short_filter), in_hbm(rates))

    rounds = count.bit_length() - 1
    made, at = (), 0
    for r, beside in enumerate(windows(groups, rounds)):
        size = 1 << r
        other = lax.ppermute(block, "seq", [(i, i ^ size) for i in range(count)])
        if beside:
            inputs = [query, gated, taps, decay, coefficient, skip, starts]
            made = pl.pallas_call(
                functools.partial(local_kernel, at, beside),
                in_specs=[whole] * len(inputs) + [whole] * len(made),
                out_specs=[whole] * 2,
                out_shape=[segs, segs],
                input_output_aliases={len(inputs) + i: i for i in range(len(made))},
                scratch_shapes=[spread],
                compiler_params=params,
                name="local",
            )(*inputs, *made)
            at += beside
        last = r == rounds - 1
        entering, *blocks = pl.pallas_call(
            functools.partial(join_kernel, size, tokens),
            in_specs=[whole] * 5,
            out_specs=[whole] * (1 if last else 2),
            out_shape=[enter_shape] if last else [enter_shape, block_shape],
            compiler_params=params,
            name="join",
        )(taps, rate, other, block, entering)
        block = None if last else blocks[0]
    conv, gate = made

    return pl.pallas_call(
        carry_kernel,
        in_specs=[whole] * 7,
        out_specs=hbm,
        out_shape=pltpu.HBM((tokens, channels), f32),
        scratch_shapes=[pltpu.VMEM((2, tokens, LANES), f32), slots, pltpu.SemaphoreType.DMA((2,))],
        compiler_params=params,
        name="carry",
    )(conv, gate, rate, decay, coefficient, skip, entering)


def solution(mesh):
    placed = (P(("groups", "seq"), None, None), P(), P(), P(), P())

    return jax.shard_map(body, mesh=mesh, in_specs=placed, out_specs=P(("groups", "seq"), None), check_vma=False)
```

time: 257 us -> 44.8 us (0.17); the launches traced: 253 us -> 44.5 us
  matrix products: 90.7 us -> 0 us
  local copies, waits for them, and re-layouts: 78.2 us -> 0.01 us
  other arithmetic: 66.9 us -> 0.05 us
  Pallas kernels: 0 us -> 28.2 us
  between operations: 13.6 us -> 0.08 us
  waiting for transfers between devices: 0.04 us -> 8.04 us
  starting transfers between devices: 2.44 us -> 8.19 us
    dot_general x3 -> x0, matrix products: 90.7 us -> none  [the longest x1 57.4 us: body(): inside = jnp.einsum('tsc,bsc->btc', toeplitz, blocks, precision=highest)]
    gather x2 -> x0, local copies, waits for them, and re-layouts: 49.1 us -> none  [body(): kernel[jnp.clip(lag_diff, 0, SUB - 1)]]
    pallas_call x0 -> x10, Pallas kernels: none -> 28.2 us  [the longest x4 11.8 us: body(): pl.pallas_call(functools.partial(local_kernel, at, beside), in_specs=[who...]
    mul x3 -> x1, other arithmetic: 17.2 us -> 0.05 us  [body(): residues * jnp.sqrt(-jnp.expm1(-2.0 * apart))]
    select_n x17 -> x0, other arithmetic: 14.7 us -> none  [the longest x16 14.6 us: step(): return jax.tree.map(lambda a, b: jnp.where(reached, a, b), new, before)]
    add x2 -> x0, local copies, waits for them, and re-layouts: 13.1 us -> none  [the longest x1 6.88 us: body(): convolved = (inside + carried_part).reshape(tok_rows, channels)]
    reduce_sum x1 -> x0, other arithmetic: 11.7 us -> none  [body(): kernel = jnp.sum(coefficient[None] * decay_lag, axis=1)]
    dynamic_update_slice x16 -> x0, other arithmetic: 10 us -> none  [body(): block_end, local_in = lax.scan(advance, jnp.zeros_like(rates), block_states)]
  transfers between devices with their start and end apart: 3 -> 4, of which waited for: 0 -> 3; matrix products, arithmetic and copies ran while one was open for 72% -> 0% of each run, Pallas kernels for 0% -> 27%
where the time goes in v3:
time: 44.8 us; the launch traced here: 44.5 us
  Pallas kernels  28.2 us (63%)
  starting transfers between devices  8.19 us (18%)
  waiting for transfers between devices  8.04 us (18%)
    pallas_call x4, Pallas kernels, body(): pl.pallas_call(functools.partial(local_kernel, at, beside), in_specs=[who...  11.8 us
    pallas_call x1, Pallas kernels, body(): pl.pallas_call(states_kernel, in_specs=[hbm] * 3, out_specs=[whole] * 8,...  9.58 us
    ppermute x4, starting transfers between devices, body(): other = lax.ppermute(block, 'seq', [(i, i ^ size) for i in range(count)])  8.19 us
    ppermute x4, waiting for transfers between devices, body(): other = lax.ppermute(block, 'seq', [(i, i ^ size) for i in range(count)])  8.04 us
    pallas_call x1, Pallas kernels, body(): pl.pallas_call(carry_kernel, in_specs=[whole] * 7, out_specs=hbm, out_sha...  6.5 us
  transfers between devices with their start and end apart: 4, of which 3 were waited for; matrix products, arithmetic and copies ran while one was open for 0% of the time, Pallas kernels for 27%

profile of v3, /device:TPU:0, one launch (start us, length us, event | category | flops | bytes accessed | tf_op | source)
XLA Modules:
  0.0 44.5 jit_solution(12608303532469041409)
XLA Ops:
  0.0 0.0 copy-start.1
  0.0 0.0 copy-start.2
  0.0 0.0 copy-start
  0.0 9.6 %states.1 = (f32[8,128,8,128]{3,2,1,0:T(8,128)S(1)}, f32[8,16,8,128]{3,2,1,0:T(8,128)S(1)}, f32[32,1024]{1,0:T(8,128)S(1)}, bf16[8,1024,128]{2,1,0:T(8,128)(2,1)...) custom-call(bf16[3,1024,1024]{2,1,0:T(8,128)(2,1)} %bitcast.7, ...), custom_call_target="tpu_custom_call" | custom-call | tf_op jit(solution)/shard_map/states/pallas_call | solution.py:341
  9.6 0.6 %collective-permute-start = (f32[32,1024]{1,0:T(8,128)S(1)}, f32[32,1024]{1,0:T(8,128)S(1)}, u32[]{:S(2)}, u32[]{:S(2)}) collective-permute-start(f32[32,1024]{1,0:T(8,128)S(1)} %get-tuple-element.41.mine_ref), channel_id=1, source_target_pairs={{0,1},{1,0},{2,3},{3,2},{4,5},{5,4},{6,7},{7,6},{8,9},{9,8},{10,11... | collective-permute-start | bytes 393224 | tf_op jit(solution)/shard_map/ppermute | solution.py:373
  10.2 1.0 %collective-permute-done.other_ref = f32[32,1024]{1,0:T(8,128)S(1)} collective-permute-done((f32[32,1024]{1,0:T(8,128)S(1)}, f32[32,1024]{1,0:T(8,128)S(1)}, u32[]{:S(2)}, u32[]{:S(2)}) %collective-permute-start) | collective-permute-done | bytes 131104 | tf_op jit(solution)/shard_map/ppermute | solution.py:373
  11.1 0.1 join.4
  11.2 2.9 %collective-permute-start.1 = (f32[32,1024]{1,0:T(8,128)S(1)}, f32[32,1024]{1,0:T(8,128)S(1)}, u32[]{:S(2)}, u32[]{:S(2)}) collective-permute-start(f32[32,1024]{1,0:T(8,128)S(1)} %get-tuple-element.43.mine_ref), channel_id=1, source_target_pairs={{0,2},{1,3},{2,0},{3,1},{4,6},{5,7},{6,4},{7,5},{8,10},{9,11},{10,... | collective-permute-start | bytes 393224 | tf_op jit(solution)/shard_map/ppermute | solution.py:373
  14.1 3.8 %collective-permute-done.1.other_ref = f32[32,1024]{1,0:T(8,128)S(1)} collective-permute-done((f32[32,1024]{1,0:T(8,128)S(1)}, f32[32,1024]{1,0:T(8,128)S(1)}, u32[]{:S(2)}, u32[]{:S(2)}) %collective-permute-start.1) | collective-permute-done | bytes 131104 | tf_op jit(solution)/shard_map/ppermute | solution.py:373
  18.0 0.1 join.5
  18.1 1.9 %collective-permute-start.2 = (f32[32,1024]{1,0:T(8,128)S(1)}, f32[32,1024]{1,0:T(8,128)S(1)}, u32[]{:S(2)}, u32[]{:S(2)}) collective-permute-start(f32[32,1024]{1,0:T(8,128)S(1)} %get-tuple-element.45.mine_ref), channel_id=1, source_target_pairs={{0,4},{1,5},{2,6},{3,7},{4,0},{5,1},{6,2},{7,3},{8,12},{9,13},{10,... | collective-permute-start | bytes 393224 | tf_op jit(solution)/shard_map/ppermute | solution.py:373
  19.9 3.2 %collective-permute-done.2.other_ref = f32[32,1024]{1,0:T(8,128)S(1)} collective-permute-done((f32[32,1024]{1,0:T(8,128)S(1)}, f32[32,1024]{1,0:T(8,128)S(1)}, u32[]{:S(2)}, u32[]{:S(2)}) %collective-permute-start.2) | collective-permute-done | bytes 131104 | tf_op jit(solution)/shard_map/ppermute | solution.py:373
  23.1 0.1 join.6
  23.2 2.8 %collective-permute-start.3 = (f32[32,1024]{1,0:T(8,128)S(1)}, f32[32,1024]{1,0:T(8,128)S(1)}, u32[]{:S(2)}, u32[]{:S(2)}) collective-permute-start(f32[32,1024]{1,0:T(8,128)S(1)} %get-tuple-element.47.mine_ref), channel_id=1, source_target_pairs={{0,8},{1,9},{2,10},{3,11},{4,12},{5,13},{6,14},{7,15},{8,0},{9,1},... | collective-permute-start | bytes 393224 | tf_op jit(solution)/shard_map/ppermute | solution.py:373
  26.0 0.0 copy-done.1
  26.0 0.0 copy-done.2
  26.1 0.0 copy-done
  26.1 1.5 %local.4 = (f32[8,128,8,128]{3,2,1,0:T(8,128)S(1)}, f32[8,128,8,128]{3,2,1,0:T(8,128)S(1)}) custom-call(bf16[8,1024,128]{2,1,0:T(8,128)(2,1)S(1)} %get-tuple-element.27.query_ref, f32[8,128,8,128]{3,2,1,0:T(8,128)S(1)} %get-tuple-element.28.gated_ref, f32[3,3,1024]{2,1,0:T(4,128)S(1)} %get-tuple-element.29.tap_ref, ...), custom_call_target="tpu_custom_call" | custom-call | tf_op jit(solution)/shard_map/local/pallas_call | solution.py:376
  27.6 4.4 %local.5 = (f32[8,128,8,128]{3,2,1,0:T(8,128)S(1)}, f32[8,128,8,128]{3,2,1,0:T(8,128)S(1)}) custom-call(bf16[8,1024,128]{2,1,0:T(8,128)(2,1)S(1)} %get-tuple-element.27.query_ref, f32[8,128,8,128]{3,2,1,0:T(8,128)S(1)} %get-tuple-element.28.gated_ref, f32[3,3,1024]{2,1,0:T(4,128)S(1)} %get-tuple-element.29.tap_ref, ...), custom_call_target="tpu_custom_call", output_to_operand_aliasing={{0}: (7, {}), {1}: (8, {})} | custom-call | tf_op jit(solution)/shard_map/local/pallas_call | solution.py:376
  32.0 3.0 %local.6 = (f32[8,128,8,128]{3,2,1,0:T(8,128)S(1)}, f32[8,128,8,128]{3,2,1,0:T(8,128)S(1)}) custom-call(bf16[8,1024,128]{2,1,0:T(8,128)(2,1)S(1)} %get-tuple-element.27.query_ref, f32[8,128,8,128]{3,2,1,0:T(8,128)S(1)} %get-tuple-element.28.gated_ref, f32[3,3,1024]{2,1,0:T(4,128)S(1)} %get-tuple-element.29.tap_ref, ...), custom_call_target="tpu_custom_call", output_to_operand_aliasing={{0}: (7, {}), {1}: (8, {})} | custom-call | tf_op jit(solution)/shard_map/local/pallas_call | solution.py:376
  35.0 3.0 %local.7 = (f32[8,128,8,128]{3,2,1,0:T(8,128)S(1)}, f32[8,128,8,128]{3,2,1,0:T(8,128)S(1)}) custom-call(bf16[8,1024,128]{2,1,0:T(8,128)(2,1)S(1)} %get-tuple-element.27.query_ref, f32[8,128,8,128]{3,2,1,0:T(8,128)S(1)} %get-tuple-element.28.gated_ref, f32[3,3,1024]{2,1,0:T(4,128)S(1)} %get-tuple-element.29.tap_ref, ...), custom_call_target="tpu_custom_call", output_to_operand_aliasing={{0}: (7, {}), {1}: (8, {})} | custom-call | tf_op jit(solution)/shard_map/local/pallas_call | solution.py:376
  38.0 0.0 collective-permute-done.3.other_ref
  38.0 6.5 %carry.1 = f32[1024,1024]{1,0:T(8,128)} custom-call(f32[8,128,8,128]{3,2,1,0:T(8,128)S(1)} %get-tuple-element.38.conv_ref, f32[8,128,8,128]{3,2,1,0:T(8,128)S(1)} %get-tuple-element.39.gate_ref, f32[16,1024]{1,0:T(8,128)S(1)} %get-tuple-element.40.rate_ref, f32[16,1024]{1,0:T(8,128)S(1)} %get-tuple-element.30.decay_ref, ...), custom_call_target="tpu_custom_call" | custom-call | tf_op jit(solution)/shard_map/carry/pallas_call | solution.py:399
  (2 shorter events, 0.1 us)
Async XLA Ops:
  0.0 26.0 %copy-start.1 = (f32[16,1024]{1,0:T(8,128)S(1)}, f32[16,1024]{1,0:T(8,128)}, u32[]{:S(2)}) copy-start(f32[16,1024]{1,0:T(8,128)} %rate_ref.1) | copy-start | bytes 196612
  0.0 26.0 %copy-start.2 = (f32[16,1024]{1,0:T(8,128)S(1)}, f32[16,1024]{1,0:T(8,128)}, u32[]{:S(2)}) copy-start(f32[16,1024]{1,0:T(8,128)} %param.7) | copy-start | bytes 196612
  0.0 26.1 %copy-start = (f32[1024]{0:T(1024)S(1)}, f32[1024]{0:T(1024)}, u32[]{:S(2)}) copy-start(f32[1024]{0:T(1024)} %param.9) | copy-start | bytes 12292
  9.6 1.6 %collective-permute-start = (f32[32,1024]{1,0:T(8,128)S(1)}, f32[32,1024]{1,0:T(8,128)S(1)}, u32[]{:S(2)}, u32[]{:S(2)}) collective-permute-start(f32[32,1024]{1,0:T(8,128)S(1)} %get-tuple-element.41.mine_ref), channel_id=1, source_target_pairs={{0,1},{1,0},{2,3},{3,2},{4,5},{5,4},{6,7},{7,6},{8,9},{9,8},{10,11... | collective-permute-start | bytes 393224 | tf_op jit(solution)/shard_map/ppermute | solution.py:373
  11.2 6.8 %collective-permute-start.1 = (f32[32,1024]{1,0:T(8,128)S(1)}, f32[32,1024]{1,0:T(8,128)S(1)}, u32[]{:S(2)}, u32[]{:S(2)}) collective-permute-start(f32[32,1024]{1,0:T(8,128)S(1)} %get-tuple-element.43.mine_ref), channel_id=1, source_target_pairs={{0,2},{1,3},{2,0},{3,1},{4,6},{5,7},{6,4},{7,5},{8,10},{9,11},{10,... | collective-permute-start | bytes 393224 | tf_op jit(solution)/shard_map/ppermute | solution.py:373
  18.1 5.1 %collective-permute-start.2 = (f32[32,1024]{1,0:T(8,128)S(1)}, f32[32,1024]{1,0:T(8,128)S(1)}, u32[]{:S(2)}, u32[]{:S(2)}) collective-permute-start(f32[32,1024]{1,0:T(8,128)S(1)} %get-tuple-element.45.mine_ref), channel_id=1, source_target_pairs={{0,4},{1,5},{2,6},{3,7},{4,0},{5,1},{6,2},{7,3},{8,12},{9,13},{10,... | collective-permute-start | bytes 393224 | tf_op jit(solution)/shard_map/ppermute | solution.py:373
  23.2 14.8 %collective-permute-start.3 = (f32[32,1024]{1,0:T(8,128)S(1)}, f32[32,1024]{1,0:T(8,128)S(1)}, u32[]{:S(2)}, u32[]{:S(2)}) collective-permute-start(f32[32,1024]{1,0:T(8,128)S(1)} %get-tuple-element.47.mine_ref), channel_id=1, source_target_pairs={{0,8},{1,9},{2,10},{3,11},{4,12},{5,13},{6,14},{7,15},{8,0},{9,1},... | collective-permute-start | bytes 393224 | tf_op jit(solution)/shard_map/ppermute | solution.py:373

commit v4 on v3

v4 whole, which is shorter than its diff:
```python
import functools

import jax
import jax.numpy as jnp
from jax import lax
from jax.experimental import pallas as pl
from jax.experimental.pallas import tpu as pltpu
from jax.sharding import PartitionSpec as P


SEG = 8
LANES = 128
CHUNK = 32
TILE = 16
RIM, HEAD = 6, 4
PITCH = CHUNK + 8
VMEM_LIMIT = 16 << 20
f32 = jnp.float32


def rows(vec):
    return jnp.broadcast_to(vec, (SEG, LANES))


def total(parts):
    while len(parts) > 1:
        tail = [parts[-1]] if len(parts) % 2 else []
        parts = [a + b for a, b in zip(parts[::2], parts[1::2])] + tail
    return parts[0]


def later(x, by):
    row = lax.broadcasted_iota(jnp.int32, x.shape, 0)
    return jnp.where(row >= by, pltpu.roll(x, by, 0), 0.0)


def each(ref, at):
    return [rows(ref[n : n + 1, at]) for n in range(ref.shape[0])]


class Spread:
    def __init__(self, block, slots, steps):
        self.block, self.slots, self.steps = block, slots, steps

    def load(self, seg, chunk, slot, tile, first=0):
        start = pl.multiple_of(seg * self.steps + chunk * CHUNK + tile * TILE, TILE)
        piece = self.block[pl.ds(start, TILE), :].astype(f32)[first:]
        self.slots[slot, pl.ds((tile * TILE + first) * SEG + seg, TILE - first, stride=SEG), :] = piece

    def at(self, slot, k):
        return self.slots[slot, pl.ds(k * SEG, SEG), :]

    def begin(self):
        tiles = CHUNK // TILE
        for seg in range(SEG):
            self.load(seg, self.steps // CHUNK - 1, 1, tiles - 1, TILE - 2)
            for tile in range(tiles):
                self.load(seg, 0, 0, tile)
        return later(self.at(1, CHUNK - 1), 1), later(self.at(1, CHUNK - 2), 1)


def spreading(parts):
    items = [(p, seg, tile) for tile in range(CHUNK // TILE) for seg in range(SEG) for p in parts]

    def ahead(u, b, coming, after):
        for p, seg, tile in items[u * len(items) // CHUNK : (u + 1) * len(items) // CHUNK]:
            p.load(seg, coming, after, tile)

    return ahead


def chunk_loop(steps, one, ahead, start):
    chunks = steps // CHUNK

    def trip(b, c):
        slot, after = lax.rem(b, 2), lax.rem(b + 1, 2)
        coming = lax.rem(b + 1, chunks)
        for u in range(CHUNK):
            c = one(b * CHUNK + u, slot, u, c)
            ahead(u, b, coming, after)
        return c

    return lax.fori_loop(0, chunks, trip, start)


def lanes(c):
    return pl.ds(pl.multiple_of(c * LANES, LANES), LANES)


def states_kernel(
    stream_ref, tap_ref, rate_ref,
    gated_ref, start_ref, send_ref, query_ref, taps_ref, tall_taps, tall_rates, rates_ref, decay_ref, enter_ref,
    raw, stride_decay, key_slots, val_slots, raw_sem, query_sem, small_sem,
):
    groups, steps = gated_ref.shape[:2]
    modes, tokens = rate_ref.shape[0], steps * SEG

    def fetch(c, slot):
        return pltpu.make_async_copy(stream_ref.at[1:3, :, lanes(c)], raw.at[slot], raw_sem.at[slot])

    def fetch_query(c):
        return pltpu.make_async_copy(stream_ref.at[0, :, lanes(c)], query_ref.at[c], query_sem.at[c])

    small = [
        pltpu.make_async_copy(rate_ref, rates_ref, small_sem.at[0]),
        pltpu.make_async_copy(tap_ref, taps_ref, small_sem.at[1]),
    ]
    fetch(0, 0).start()
    for copy in small:
        copy.start()
    for copy in small:
        copy.wait()
    decay_ref[...] = jnp.exp(-rates_ref[...])
    stride_decay[...] = jnp.exp(-rates_ref[...] * float(steps))
    enter_ref[...] = jnp.zeros_like(enter_ref)

    def group(c, _):
        slot = lax.rem(c, 2)

        @pl.when(c + 1 < groups)
        def _():
            fetch(c + 1, 1 - slot).start()

        fetch_query(c).start()
        fetch(c, slot).wait()
        keys = Spread(raw.at[slot, 0], key_slots, steps)
        vals = Spread(raw.at[slot, 1], val_slots, steps)
        at, row = lanes(c), pl.ds(c, 1)
        taps = [[rows(taps_ref[d, j : j + 1, at]) for d in range(3)] for j in (1, 2)]
        decay = each(decay_ref, at)
        before = [*keys.begin(), *vals.begin()]

        def one(k, slot, u, carried):
            k1, k2, v1, v2, *state = carried
            k0, v0 = keys.at(slot, u), vals.at(slot, u)
            a = taps[0][0] * k0 + taps[0][1] * k1 + taps[0][2] * k2
            b = taps[1][0] * v0 + taps[1][1] * v1 + taps[1][2] * v2
            x = a * b
            gated_ref[c, k] = x
            return (k0, k1, v0, v1, *[d * s + x for d, s in zip(decay, state)])

        zero = jnp.zeros((SEG, LANES), f32)
        final = chunk_loop(steps, one, spreading((keys, vals)), (*before, *[zero] * modes))[4:]
        for n, d in enumerate(each(stride_decay, at)):
            s = final[n]
            for by in (1, 2, 4):
                s = s + d * later(s, by)
                d = d * d
            start_ref[c, n] = later(s, 1)
            send_ref[n, row, :] = s[SEG - 1 : SEG, :]
            tall_rates[n, row, :] = rates_ref[n : n + 1, at]
        for j in range(3):
            for d in range(3):
                tall_taps[3 * j + d, row, :] = taps_ref[d, j : j + 1, at]
        for j in range(2):
            rim = raw[slot, j, tokens - TILE :, :].astype(f32)[TILE - 2 :]
            head = raw[slot, j, :TILE, :].astype(f32)[:2]
            for t in range(2):
                send_ref[modes + 2 * j + t, row, :] = rim[t : t + 1]
                send_ref[modes + RIM + 2 * j + t, row, :] = head[t : t + 1]
                enter_ref[modes + 4 + 2 * j + t, row, :] = head[t : t + 1]
        return 0

    lax.fori_loop(0, groups, group, 0)

    def landed(c, _):
        fetch_query(c).wait()
        rim = query_ref[c, tokens - TILE :, :].astype(f32)[TILE - 2 :]
        for t in range(2):
            send_ref[modes + 4 + t, pl.ds(c, 1), :] = rim[t : t + 1]
        return 0

    lax.fori_loop(0, groups, landed, 0)


def join_kernel(size, tokens, last, tap_ref, rate_ref, coef_ref, skip_ref, other_ref, mine_ref, enter_ref, enter_out, *mine_out):
    modes = rate_ref.shape[0]
    rim_at, change_at, head_at = modes, modes, modes + 4
    place = lax.axis_index("seq")
    second = (place & size) != 0
    rate = rate_ref[...]

    def after(times):
        return jnp.exp(-rate * times)

    def change(rim, head):
        w = [[tap_ref[3 * j + d] for d in range(3)] for j in (1, 2, 0)]
        more0 = [w[j][1] * rim[2 * j + 1] + w[j][2] * rim[2 * j] for j in range(3)]
        more1 = [w[j][2] * rim[2 * j + 1] for j in range(3)]
        own0 = [w[j][0] * head[2 * j] for j in range(2)]
        own1 = [w[j][0] * head[2 * j + 1] + w[j][1] * head[2 * j] for j in range(2)]
        change0 = (own0[0] + more0[0]) * (own0[1] + more0[1]) - own0[0] * own0[1]
        change1 = (own1[0] + more1[0]) * (own1[1] + more1[1]) - own1[0] * own1[1]
        return change0, change1, more0[2], more1[2]

    def merge(early, late, change0, change1, head_ref, head_from):
        span = float(tokens * size)
        out = mine_out[0]
        out[:modes] = late[:modes] + after(span) * early[:modes] + after(span - 1.0) * change0 + after(span - 2.0) * change1
        out[rim_at : rim_at + RIM] = late[rim_at : rim_at + RIM]
        head = head_ref[head_from : head_from + HEAD]
        enter_out[head_at : head_at + HEAD] = head
        if out.shape[0] > modes + RIM:
            out[rim_at + RIM :] = head

    @pl.when(second)
    def _():
        edge = change(other_ref[rim_at : rim_at + RIM], enter_ref[head_at : head_at + HEAD])
        before = place & (size - 1)
        span = before.astype(f32) * float(tokens)
        enter_out[:modes] = (
            enter_ref[:modes] + after(span) * other_ref[:modes] + after(span - 1.0) * edge[0] + after(span - 2.0) * edge[1]
        )
        enter_out[change_at:] = enter_ref[change_at:]

        @pl.when(before == 0)
        def _():
            for i, row in enumerate(edge):
                enter_out[change_at + i] = row

        if not last:
            merge(other_ref, mine_ref, *edge[:2], other_ref, rim_at + RIM)

    @pl.when(jnp.logical_not(second))
    def _():
        enter_out[...] = enter_ref[...]
        if not last:
            edge = change(mine_ref[rim_at : rim_at + RIM], other_ref[rim_at + RIM : rim_at + RIM + HEAD])
            merge(mine_ref, other_ref, *edge[:2], enter_ref, head_at)

    if last:
        coef, skip = coef_ref[...], skip_ref[0]
        weight = coef * enter_out[:modes]
        change0, change1 = enter_out[change_at], enter_out[change_at + 1]
        once = after(1.0)
        enter_out[:modes] = weight
        enter_out[change_at] = skip * change0 + jnp.sum(weight * once - coef * (after(-1.0) * change1), axis=0)
        enter_out[change_at + 1] = skip * change1 + jnp.sum(weight * (once * once), axis=0)


def local_kernel(at, beside, query_ref, gated_ref, tap_ref, decay_ref, coef_ref, skip_ref, start_ref, *rest):
    conv_ref, gate_ref, slots = rest[-3:]
    steps = gated_ref.shape[1]
    modes = decay_ref.shape[0]

    def group(i, _):
        c = i + at
        on = lanes(c)
        queries = Spread(query_ref.at[c], slots, steps)
        taps = [rows(tap_ref[d, 0:1, on]) for d in range(3)]
        decay = each(decay_ref, on)
        coef = [rows(coef_ref[n, pl.ds(c, 1), :]) for n in range(modes)]
        skip = rows(skip_ref[0, pl.ds(c, 1), :])
        before = queries.begin()

        def one(k, slot, u, carried):
            q1, q2, *state = carried
            q0, x = queries.at(slot, u), gated_ref[c, k]
            gate_ref[c, k] = taps[0] * q0 + taps[1] * q1 + taps[2] * q2
            state = [d * s + x for d, s in zip(decay, state)]
            conv_ref[c, k] = total([a * s for a, s in zip(coef, state)] + [skip * x])
            return (q0, q1, *state)

        chunk_loop(steps, one, spreading((queries,)), (*before, *[start_ref[c, n] for n in range(modes)]))
        return 0

    lax.fori_loop(0, beside, group, 0)


def carry_kernel(conv_ref, gate_ref, rate_ref, decay_ref, enter_ref, out_ref, mixed, slots, sem):
    groups, steps = conv_ref.shape[:2]
    modes, chunks = rate_ref.shape[0], steps // CHUNK

    def store(c, side):
        return pltpu.make_async_copy(mixed.at[side], out_ref.at[:, lanes(c)], sem.at[side])

    def group(c, _):
        side, on = lax.rem(c, 2), lanes(c)

        @pl.when(c >= 2)
        def _():
            store(c - 2, side).wait()

        row = pl.ds(c, 1)
        decay = each(decay_ref, on)
        first = lax.broadcasted_iota(jnp.int32, (SEG, LANES), 0).astype(f32) * steps
        part = [jnp.exp(-rows(rate_ref[n : n + 1, on]) * first) * rows(enter_ref[n, row, :]) for n in range(modes)]

        def one(k, slot, u, part):
            part = [d * s for d, s in zip(decay, part)]
            slots[slot, pl.ds(u, SEG, stride=PITCH), :] = gate_ref[c, k] * (conv_ref[c, k] + total(part))
            return part

        def put(seg, chunk, slot, tile):
            start = pl.multiple_of(seg * steps + chunk * CHUNK + tile * TILE, TILE)
            mixed[side, pl.ds(start, TILE), :] = slots[slot, pl.ds(seg * PITCH + tile * TILE, TILE), :]

        items = [(seg, tile) for tile in range(CHUNK // TILE) for seg in range(SEG)]

        def ahead(u, b, coming, after):
            for seg, tile in items[u * len(items) // CHUNK : (u + 1) * len(items) // CHUNK]:
                put(seg, jnp.maximum(b - 1, 0), after, tile)

        chunk_loop(steps, one, ahead, part)
        for seg, tile in items:
            put(seg, chunks - 1, (chunks - 1) % 2, tile)

        for t in range(2):
            gate = gate_ref[c, t, 0:1, :] + enter_ref[modes + 2 + t, row, :]
            mixed[side, t : t + 1, :] = gate * (conv_ref[c, t, 0:1, :] + enter_ref[modes + t, row, :])
        store(c, side).start()
        return 0

    lax.fori_loop(0, groups, group, 0)
    for c in range(max(groups - 2, 0), groups):
        store(c, c % 2).wait()


def in_hbm(x):
    return pltpu.with_memory_space_constraint(x, pltpu.HBM)


def windows(groups, rounds):
    counts = [0] * rounds
    order = [*range(1, rounds), 0]
    for i in range(groups):
        counts[order[i % rounds] if i < rounds else 1 + (i - rounds) % (rounds - 1)] += 1
    return counts


def body(streams, short_filter, residues, rates, skip):
    tokens, _, channels = streams.shape
    modes = rates.shape[0]
    steps = tokens // SEG
    groups = channels // LANES
    count = lax.axis_size("seq")
    assert count & (count - 1) == 0 and tokens % (SEG * CHUNK * 2) == 0

    by_stream = in_hbm(jnp.transpose(streams, (1, 0, 2)))
    apart = lax.optimization_barrier(rates)
    coefficient = lax.optimization_barrier(residues * jnp.sqrt(-jnp.expm1(-2.0 * apart)))
    coefficient = coefficient.reshape(modes, groups, LANES)
    skip = skip.reshape(1, groups, LANES)

    segs = pltpu.VMEM((groups, steps, SEG, LANES), f32)
    spread = pltpu.VMEM((2, SEG * CHUNK, LANES), f32)
    slots = pltpu.VMEM((2, SEG * PITCH, LANES), f32)
    hbm = pl.BlockSpec(memory_space=pltpu.HBM)
    whole = pl.BlockSpec(memory_space=pltpu.VMEM)
    params = pltpu.CompilerParams(vmem_limit_bytes=VMEM_LIMIT)

    def tall(count):
        return pltpu.VMEM((count, groups, LANES), f32)

    enter_shape = tall(modes + 4 + HEAD)
    mode_shape = pltpu.VMEM((modes, channels), f32)

    gated, starts, block, query, taps, tall_taps, tall_rate, rate, decay, entering = pl.pallas_call(
        states_kernel,
        in_specs=[hbm] * 3,
        out_specs=[whole] * 10,
        out_shape=[
            segs,
            pltpu.VMEM((groups, modes, SEG, LANES), f32),
            tall(modes + RIM + HEAD),
            pltpu.VMEM((groups, tokens, LANES), streams.dtype),
            pltpu.VMEM(short_filter.shape, f32),
            tall(9),
            tall(modes),
            mode_shape,
            mode_shape,
            enter_shape,
        ],
        scratch_shapes=[
            pltpu.VMEM((2, 2, tokens, LANES), streams.dtype),
            mode_shape,
            spread,
            spread,
            pltpu.SemaphoreType.DMA((2,)),
            pltpu.SemaphoreType.DMA((groups,)),
            pltpu.SemaphoreType.DMA((2,)),
        ],
        compiler_params=params,
        name="states",
    )(by_stream, in_hbm(short_filter), in_hbm(rates))

    rounds = count.bit_length() - 1
    made, at = (), 0
    for r, beside in enumerate(windows(groups, rounds)):
        size = 1 << r
        other = lax.ppermute(block, "seq", [(i, i ^ size) for i in range(count)])
        if beside:
            inputs = [query, gated, taps, decay, coefficient, skip, starts]
            made = pl.pallas_call(
                functools.partial(local_kernel, at, beside),
                in_specs=[whole] * len(inputs) + [whole] * len(made),
                out_specs=[whole] * 2,
                out_shape=[segs, segs],
                input_output_aliases={len(inputs) + i: i for i in range(len(made))},
                scratch_shapes=[spread],
                compiler_params=params,
                name="local",
            )(*inputs, *made)
            at += beside
        last = r == rounds - 1
        sent = tall(modes + RIM + (0 if r == rounds - 2 else HEAD))
        entering, *blocks = pl.pallas_call(
            functools.partial(join_kernel, size, tokens, last),
            in_specs=[whole] * 7,
            out_specs=[whole] * (1 if last else 2),
            out_shape=[enter_shape] if last else [enter_shape, sent],
            compiler_params=params,
            name="join",
        )(tall_taps, tall_rate, coefficient, skip, other, block, entering)
        block = None if last else blocks[0]
    conv, gate = made

    return pl.pallas_call(
        carry_kernel,
        in_specs=[whole] * 5,
        out_specs=hbm,
        out_shape=pltpu.HBM((tokens, channels), f32),
        scratch_shapes=[pltpu.VMEM((2, tokens, LANES), f32), slots, pltpu.SemaphoreType.DMA((2,))],
        compiler_params=params,
        name="carry",
    )(conv, gate, rate, decay, entering)


def solution(mesh):
    placed = (P(("groups", "seq"), None, None), P(), P(), P(), P())

    return jax.shard_map(body, mesh=mesh, in_specs=placed, out_specs=P(("groups", "seq"), None), check_vma=False)
```

time: 44.8 us -> 43.6 us (0.973)
  waiting for transfers between devices: 8.04 us -> 7.11 us
    ppermute x4, waiting for transfers between devices: 8.04 us -> 7.11 us  [body(): other = lax.ppermute(block, 'seq', [(i, i ^ size) for i in range(count)])]
where the time goes in v4:
time: 43.6 us; the launch traced here: 43.4 us
  Pallas kernels  27.9 us (64%)
  starting transfers between devices  8.23 us (19%)
  waiting for transfers between devices  7.11 us (16%)
    pallas_call x4, Pallas kernels, body(): pl.pallas_call(functools.partial(local_kernel, at, beside), in_specs=[who...  11.9 us
    pallas_call x1, Pallas kernels, body(): pl.pallas_call(states_kernel, in_specs=[hbm] * 3, out_specs=[whole] * 10,...  9.41 us
    ppermute x4, starting transfers between devices, body(): other = lax.ppermute(block, 'seq', [(i, i ^ size) for i in range(count)])  8.23 us
    ppermute x4, waiting for transfers between devices, body(): other = lax.ppermute(block, 'seq', [(i, i ^ size) for i in range(count)])  7.11 us
    pallas_call x1, Pallas kernels, body(): pl.pallas_call(carry_kernel, in_specs=[whole] * 5, out_specs=hbm, out_sha...  6.38 us
  transfers between devices with their start and end apart: 4, of which 3 were waited for; matrix products, arithmetic and copies ran while one was open for 0% of the time, Pallas kernels for 27%

profile of v4, /device:TPU:0, one launch (start us, length us, event | category | flops | bytes accessed | tf_op | source)
XLA Modules:
  0.0 43.4 jit_solution(16782042937348145892)
XLA Ops:
  0.0 0.0 copy-start.1
  0.0 0.0 copy-start.2
  0.0 0.0 copy-start
  0.0 9.4 %states.1 = (f32[8,128,8,128]{3,2,1,0:T(8,128)S(1)}, f32[8,16,8,128]{3,2,1,0:T(8,128)S(1)}, f32[26,8,128]{2,1,0:T(8,128)S(1)}, bf16[8,1024,128]{2,1,0:T(8,128)(2...) custom-call(bf16[3,1024,1024]{2,1,0:T(8,128)(2,1)} %bitcast.20, ...), custom_call_target="tpu_custom_call" | custom-call | tf_op jit(solution)/shard_map/states/pallas_call | solution.py:358
  9.4 0.6 %collective-permute-start = (f32[26,8,128]{2,1,0:T(8,128)S(1)}, f32[26,8,128]{2,1,0:T(8,128)S(1)}, u32[]{:S(2)}, u32[]{:S(2)}) collective-permute-start(f32[26,8,128]{2,1,0:T(8,128)S(1)} %get-tuple-element.45.mine_ref), channel_id=1, source_target_pairs={{0,1},{1,0},{2,3},{3,2},{4,5},{5,4},{6,7},{7,6},{8,9},{9,8},{10,11... | collective-permute-start | bytes 319496 | tf_op jit(solution)/shard_map/ppermute | solution.py:391
  10.0 0.0 copy-done.1
  10.0 0.0 copy-done.2
  10.1 0.9 %collective-permute-done.other_ref = f32[26,8,128]{2,1,0:T(8,128)S(1)} collective-permute-done((f32[26,8,128]{2,1,0:T(8,128)S(1)}, f32[26,8,128]{2,1,0:T(8,128)S(1)}, u32[]{:S(2)}, u32[]{:S(2)}) %collective-permute-start) | collective-permute-done | bytes 106528 | tf_op jit(solution)/shard_map/ppermute | solution.py:391
  10.9 0.0 copy-done
  10.9 0.1 join.4
  11.0 2.9 %collective-permute-start.1 = (f32[26,8,128]{2,1,0:T(8,128)S(1)}, f32[26,8,128]{2,1,0:T(8,128)S(1)}, u32[]{:S(2)}, u32[]{:S(2)}) collective-permute-start(f32[26,8,128]{2,1,0:T(8,128)S(1)} %get-tuple-element.47.mine_ref), channel_id=1, source_target_pairs={{0,2},{1,3},{2,0},{3,1},{4,6},{5,7},{6,4},{7,5},{8,10},{9,11},{10,... | collective-permute-start | bytes 319496 | tf_op jit(solution)/shard_map/ppermute | solution.py:391
  13.9 3.3 %collective-permute-done.1.other_ref = f32[26,8,128]{2,1,0:T(8,128)S(1)} collective-permute-done((f32[26,8,128]{2,1,0:T(8,128)S(1)}, f32[26,8,128]{2,1,0:T(8,128)S(1)}, u32[]{:S(2)}, u32[]{:S(2)}) %collective-permute-start.1) | collective-permute-done | bytes 106528 | tf_op jit(solution)/shard_map/ppermute | solution.py:391
  17.3 0.1 join.5
  17.3 1.9 %collective-permute-start.2 = (f32[26,8,128]{2,1,0:T(8,128)S(1)}, f32[26,8,128]{2,1,0:T(8,128)S(1)}, u32[]{:S(2)}, u32[]{:S(2)}) collective-permute-start(f32[26,8,128]{2,1,0:T(8,128)S(1)} %get-tuple-element.49.mine_ref), channel_id=1, source_target_pairs={{0,4},{1,5},{2,6},{3,7},{4,0},{5,1},{6,2},{7,3},{8,12},{9,13},{10,... | collective-permute-start | bytes 319496 | tf_op jit(solution)/shard_map/ppermute | solution.py:391
  19.2 2.9 %collective-permute-done.2.other_ref = f32[26,8,128]{2,1,0:T(8,128)S(1)} collective-permute-done((f32[26,8,128]{2,1,0:T(8,128)S(1)}, f32[26,8,128]{2,1,0:T(8,128)S(1)}, u32[]{:S(2)}, u32[]{:S(2)}) %collective-permute-start.2) | collective-permute-done | bytes 106528 | tf_op jit(solution)/shard_map/ppermute | solution.py:391
  22.1 0.1 join.6
  22.1 2.9 %collective-permute-start.3 = (f32[22,8,128]{2,1,0:T(8,128)S(1)}, f32[22,8,128]{2,1,0:T(8,128)S(1)}, u32[]{:S(2)}, u32[]{:S(2)}) collective-permute-start(f32[22,8,128]{2,1,0:T(8,128)S(1)} %get-tuple-element.51.mine_ref), channel_id=1, source_target_pairs={{0,8},{1,9},{2,10},{3,11},{4,12},{5,13},{6,14},{7,15},{8,0},{9,1},... | collective-permute-start | bytes 270344 | tf_op jit(solution)/shard_map/ppermute | solution.py:391
  25.0 1.5 %local.4 = (f32[8,128,8,128]{3,2,1,0:T(8,128)S(1)}, f32[8,128,8,128]{3,2,1,0:T(8,128)S(1)}) custom-call(bf16[8,1024,128]{2,1,0:T(8,128)(2,1)S(1)} %get-tuple-element.29.query_ref, f32[8,128,8,128]{3,2,1,0:T(8,128)S(1)} %get-tuple-element.30.gated_ref, f32[3,3,1024]{2,1,0:T(4,128)S(1)} %get-tuple-element.31.tap_ref, ...), custom_call_target="tpu_custom_call" | custom-call | tf_op jit(solution)/shard_map/local/pallas_call | solution.py:394
  26.5 4.5 %local.5 = (f32[8,128,8,128]{3,2,1,0:T(8,128)S(1)}, f32[8,128,8,128]{3,2,1,0:T(8,128)S(1)}) custom-call(bf16[8,1024,128]{2,1,0:T(8,128)(2,1)S(1)} %get-tuple-element.29.query_ref, f32[8,128,8,128]{3,2,1,0:T(8,128)S(1)} %get-tuple-element.30.gated_ref, f32[3,3,1024]{2,1,0:T(4,128)S(1)} %get-tuple-element.31.tap_ref, ...), custom_call_target="tpu_custom_call", output_to_operand_aliasing={{0}: (7, {}), {1}: (8, {})} | custom-call | tf_op jit(solution)/shard_map/local/pallas_call | solution.py:394
  31.0 3.0 %local.6 = (f32[8,128,8,128]{3,2,1,0:T(8,128)S(1)}, f32[8,128,8,128]{3,2,1,0:T(8,128)S(1)}) custom-call(bf16[8,1024,128]{2,1,0:T(8,128)(2,1)S(1)} %get-tuple-element.29.query_ref, f32[8,128,8,128]{3,2,1,0:T(8,128)S(1)} %get-tuple-element.30.gated_ref, f32[3,3,1024]{2,1,0:T(4,128)S(1)} %get-tuple-element.31.tap_ref, ...), custom_call_target="tpu_custom_call", output_to_operand_aliasing={{0}: (7, {}), {1}: (8, {})} | custom-call | tf_op jit(solution)/shard_map/local/pallas_call | solution.py:394
  33.9 3.0 %local.7 = (f32[8,128,8,128]{3,2,1,0:T(8,128)S(1)}, f32[8,128,8,128]{3,2,1,0:T(8,128)S(1)}) custom-call(bf16[8,1024,128]{2,1,0:T(8,128)(2,1)S(1)} %get-tuple-element.29.query_ref, f32[8,128,8,128]{3,2,1,0:T(8,128)S(1)} %get-tuple-element.30.gated_ref, f32[3,3,1024]{2,1,0:T(4,128)S(1)} %get-tuple-element.31.tap_ref, ...), custom_call_target="tpu_custom_call", output_to_operand_aliasing={{0}: (7, {}), {1}: (8, {})} | custom-call | tf_op jit(solution)/shard_map/local/pallas_call | solution.py:394
  36.9 0.0 collective-permute-done.3.other_ref
  36.9 0.1 join.7.enter_ref
  37.0 6.4 %carry.1 = f32[1024,1024]{1,0:T(8,128)} custom-call(f32[8,128,8,128]{3,2,1,0:T(8,128)S(1)} %get-tuple-element.40.conv_ref, f32[8,128,8,128]{3,2,1,0:T(8,128)S(1)} %get-tuple-element.41.gate_ref, f32[16,1024]{1,0:T(8,128)S(1)} %get-tuple-element.42.rate_ref, f32[16,1024]{1,0:T(8,128)S(1)} %get-tuple-element.32.decay_ref, f32[24,8,128]{2,1,0:T(8,128)S(1)} %join.7.enter_ref), custom_call_target="tpu_custom_call" | custom-call | tf_op jit(solution)/shard_map/carry/pallas_call | solution.py:418
  (2 shorter events, 0.1 us)
Async XLA Ops:
  0.0 10.0 %copy-start.1 = (f32[16,1024]{1,0:T(8,128)S(1)}, f32[16,1024]{1,0:T(8,128)}, u32[]{:S(2)}) copy-start(f32[16,1024]{1,0:T(8,128)} %rate_ref.1) | copy-start | bytes 196612
  0.0 10.0 %copy-start.2 = (f32[16,1024]{1,0:T(8,128)S(1)}, f32[16,1024]{1,0:T(8,128)}, u32[]{:S(2)}) copy-start(f32[16,1024]{1,0:T(8,128)} %param.7) | copy-start | bytes 196612
  0.0 10.9 %copy-start = (f32[1024]{0:T(1024)S(1)}, f32[1024]{0:T(1024)}, u32[]{:S(2)}) copy-start(f32[1024]{0:T(1024)} %param.9) | copy-start | bytes 12292
  9.4 1.5 %collective-permute-start = (f32[26,8,128]{2,1,0:T(8,128)S(1)}, f32[26,8,128]{2,1,0:T(8,128)S(1)}, u32[]{:S(2)}, u32[]{:S(2)}) collective-permute-start(f32[26,8,128]{2,1,0:T(8,128)S(1)} %get-tuple-element.45.mine_ref), channel_id=1, source_target_pairs={{0,1},{1,0},{2,3},{3,2},{4,5},{5,4},{6,7},{7,6},{8,9},{9,8},{10,11... | collective-permute-start | bytes 319496 | tf_op jit(solution)/shard_map/ppermute | solution.py:391
  11.0 6.2 %collective-permute-start.1 = (f32[26,8,128]{2,1,0:T(8,128)S(1)}, f32[26,8,128]{2,1,0:T(8,128)S(1)}, u32[]{:S(2)}, u32[]{:S(2)}) collective-permute-start(f32[26,8,128]{2,1,0:T(8,128)S(1)} %get-tuple-element.47.mine_ref), channel_id=1, source_target_pairs={{0,2},{1,3},{2,0},{3,1},{4,6},{5,7},{6,4},{7,5},{8,10},{9,11},{10,... | collective-permute-start | bytes 319496 | tf_op jit(solution)/shard_map/ppermute | solution.py:391
  17.3 4.8 %collective-permute-start.2 = (f32[26,8,128]{2,1,0:T(8,128)S(1)}, f32[26,8,128]{2,1,0:T(8,128)S(1)}, u32[]{:S(2)}, u32[]{:S(2)}) collective-permute-start(f32[26,8,128]{2,1,0:T(8,128)S(1)} %get-tuple-element.49.mine_ref), channel_id=1, source_target_pairs={{0,4},{1,5},{2,6},{3,7},{4,0},{5,1},{6,2},{7,3},{8,12},{9,13},{10,... | collective-permute-start | bytes 319496 | tf_op jit(solution)/shard_map/ppermute | solution.py:391
  22.1 14.8 %collective-permute-start.3 = (f32[22,8,128]{2,1,0:T(8,128)S(1)}, f32[22,8,128]{2,1,0:T(8,128)S(1)}, u32[]{:S(2)}, u32[]{:S(2)}) collective-permute-start(f32[22,8,128]{2,1,0:T(8,128)S(1)} %get-tuple-element.51.mine_ref), channel_id=1, source_target_pairs={{0,8},{1,9},{2,10},{3,11},{4,12},{5,13},{6,14},{7,15},{8,0},{9,1},... | collective-permute-start | bytes 270344 | tf_op jit(solution)/shard_map/ppermute | solution.py:391

commit v5 on v4

--- a/solution.py
+++ b/solution.py
@@ -10,11 +10,10 @@
 
 SEG = 8
 LANES = 128
-CHUNK = 32
-TILE = 16
+CHUNK = 16
 RIM, HEAD = 6, 4
 PITCH = CHUNK + 8
-VMEM_LIMIT = 16 << 20
+VMEM_LIMIT = 20 << 20
 f32 = jnp.float32
 
 
@@ -39,74 +38,72 @@
 
 
 class Spread:
-    def __init__(self, block, slots, steps):
-        self.block, self.slots, self.steps = block, slots, steps
-
-    def load(self, seg, chunk, slot, tile, first=0):
-        start = pl.multiple_of(seg * self.steps + chunk * CHUNK + tile * TILE, TILE)
-        piece = self.block[pl.ds(start, TILE), :].astype(f32)[first:]
-        self.slots[slot, pl.ds((tile * TILE + first) * SEG + seg, TILE - first, stride=SEG), :] = piece
-
-    def at(self, slot, k):
-        return self.slots[slot, pl.ds(k * SEG, SEG), :]
+    def __init__(self, block, group, buffers, steps):
+        self.block, self.group, self.buffers, self.steps = block, group, buffers, steps
+
+    def load(self, seg, chunk, side, first=0, group=None):
+        start = pl.multiple_of(seg * self.steps + chunk * CHUNK, CHUNK)
+        on = lanes(self.group if group is None else group)
+        piece = self.block[pl.ds(start, CHUNK), on].astype(f32)[first:]
+        self.buffers[side][pl.ds(first * SEG + seg, CHUNK - first, stride=SEG), :] = piece
+
+    def at(self, side, k):
+        return self.buffers[side][pl.ds(k * SEG, SEG), :]
 
     def begin(self):
-        tiles = CHUNK // TILE
         for seg in range(SEG):
-            self.load(seg, self.steps // CHUNK - 1, 1, tiles - 1, TILE - 2)
-            for tile in range(tiles):
-                self.load(seg, 0, 0, tile)
+            self.load(seg, 0, 0)
+
+    def before(self):
+        for seg in range(SEG):
+            self.load(seg, self.steps // CHUNK - 1, 1, CHUNK - 2)
         return later(self.at(1, CHUNK - 1), 1), later(self.at(1, CHUNK - 2), 1)
 
 
-def spreading(parts):
-    items = [(p, seg, tile) for tile in range(CHUNK // TILE) for seg in range(SEG) for p in parts]
-
-    def ahead(u, b, coming, after):
-        for p, seg, tile in items[u * len(items) // CHUNK : (u + 1) * len(items) // CHUNK]:
-            p.load(seg, coming, after, tile)
-
-    return ahead
-
-
-def chunk_loop(steps, one, ahead, start):
-    chunks = steps // CHUNK
-
+def chunk_loop(steps, one, ahead, items, start, begin=0, end=None, first=None):
     def trip(b, c):
-        slot, after = lax.rem(b, 2), lax.rem(b + 1, 2)
-        coming = lax.rem(b + 1, chunks)
-        for u in range(CHUNK):
-            c = one(b * CHUNK + u, slot, u, c)
-            ahead(u, b, coming, after)
+        if first is not None:
+            first(b)
+        for side in range(2):
+            for u in range(CHUNK):
+                c = one((2 * b + side) * CHUNK + u, side, u, c)
+                for item in items[u * len(items) // CHUNK : (u + 1) * len(items) // CHUNK]:
+                    ahead(*item, 2 * b + side, 1 - side)
         return c
 
-    return lax.fori_loop(0, chunks, trip, start)
+    return lax.fori_loop(begin, steps // (2 * CHUNK) if end is None else end, trip, start)
 
 
 def lanes(c):
-    return pl.ds(pl.multiple_of(c * LANES, LANES), LANES)
+    return pl.ds(pl.multiple_of(c * LANES, LANES) if not isinstance(c, int) else c * LANES, LANES)
 
 
 def states_kernel(
     stream_ref, tap_ref, rate_ref,
     gated_ref, start_ref, send_ref, query_ref, taps_ref, tall_taps, tall_rates, rates_ref, decay_ref, enter_ref,
-    raw, stride_decay, key_slots, val_slots, raw_sem, query_sem, small_sem,
+    raw, stride_decay, *rest,
 ):
+    buffers, (raw_sem, query_sem, small_sem) = (rest[:2], rest[2:4]), rest[4:]
     groups, steps = gated_ref.shape[:2]
-    modes, tokens = rate_ref.shape[0], steps * SEG
-
-    def fetch(c, slot):
-        return pltpu.make_async_copy(stream_ref.at[1:3, :, lanes(c)], raw.at[slot], raw_sem.at[slot])
-
-    def fetch_query(c):
-        return pltpu.make_async_copy(stream_ref.at[0, :, lanes(c)], query_ref.at[c], query_sem.at[c])
+    modes, tokens, chunks = rate_ref.shape[0], steps * SEG, steps // CHUNK
+
+    edges = [0, *[1 << i for i in range(groups.bit_length())]]
+    edges = [*[e for e in edges if e < groups], groups]
+    fetches = []
+    for i, (begin, end) in enumerate(zip(edges, edges[1:])):
+        on = pl.ds(begin * LANES, (end - begin) * LANES)
+        fetches.append(pltpu.make_async_copy(stream_ref.at[1:3, :, on], raw.at[:, :, on], raw_sem.at[i]))
+    fetch_query = pltpu.make_async_copy(stream_ref.at[0], query_ref, query_sem)
+
+    def spreads(c):
+        return [Spread(raw.at[j], c, buffers[j], steps) for j in range(2)]
 
     small = [
         pltpu.make_async_copy(rate_ref, rates_ref, small_sem.at[0]),
         pltpu.make_async_copy(tap_ref, taps_ref, small_sem.at[1]),
     ]
-    fetch(0, 0).start()
-    for copy in small:
+    fetches[0].start()
+    for copy in (*small, *fetches[1:], fetch_query):
         copy.start()
     for copy in small:
         copy.wait()
@@ -114,33 +111,40 @@
     stride_decay[...] = jnp.exp(-rates_ref[...] * float(steps))
     enter_ref[...] = jnp.zeros_like(enter_ref)
 
+    fetches[0].wait()
+    for part in spreads(0):
+        part.begin()
+
     def group(c, _):
-        slot = lax.rem(c, 2)
-
-        @pl.when(c + 1 < groups)
-        def _():
-            fetch(c + 1, 1 - slot).start()
-
-        fetch_query(c).start()
-        fetch(c, slot).wait()
-        keys = Spread(raw.at[slot, 0], key_slots, steps)
-        vals = Spread(raw.at[slot, 1], val_slots, steps)
+        def next_landed(b):
+            for begin, copy in zip(edges[1:-1], fetches[1:]):
+
+                @pl.when((b + 1 == chunks // 2) & (c + 1 == begin))
+                def _():
+                    copy.wait()
+
+        parts = keys, vals = spreads(c)
         at, row = lanes(c), pl.ds(c, 1)
         taps = [[rows(taps_ref[d, j : j + 1, at]) for d in range(3)] for j in (1, 2)]
         decay = each(decay_ref, at)
-        before = [*keys.begin(), *vals.begin()]
-
-        def one(k, slot, u, carried):
+        before = [*keys.before(), *vals.before()]
+
+        def one(k, side, u, carried):
             k1, k2, v1, v2, *state = carried
-            k0, v0 = keys.at(slot, u), vals.at(slot, u)
+            k0, v0 = keys.at(side, u), vals.at(side, u)
             a = taps[0][0] * k0 + taps[0][1] * k1 + taps[0][2] * k2
             b = taps[1][0] * v0 + taps[1][1] * v1 + taps[1][2] * v2
             x = a * b
             gated_ref[c, k] = x
             return (k0, k1, v0, v1, *[d * s + x for d, s in zip(decay, state)])
 
+        def ahead(j, seg, chunk, side):
+            group = jnp.where(chunk + 1 == chunks, lax.rem(c + 1, groups), c) if side == 0 else None
+            parts[j].load(seg, lax.rem(chunk + 1, chunks), side, group=group)
+
         zero = jnp.zeros((SEG, LANES), f32)
-        final = chunk_loop(steps, one, spreading((keys, vals)), (*before, *[zero] * modes))[4:]
+        items = [(j, seg) for seg in range(SEG) for j in range(2)]
+        final = chunk_loop(steps, one, ahead, items, (*before, *[zero] * modes), first=next_landed)[4:]
         for n, d in enumerate(each(stride_decay, at)):
             s = final[n]
             for by in (1, 2, 4):
@@ -153,8 +157,8 @@
             for d in range(3):
                 tall_taps[3 * j + d, row, :] = taps_ref[d, j : j + 1, at]
         for j in range(2):
-            rim = raw[slot, j, tokens - TILE :, :].astype(f32)[TILE - 2 :]
-            head = raw[slot, j, :TILE, :].astype(f32)[:2]
+            rim = raw[j, tokens - CHUNK :, at].astype(f32)[CHUNK - 2 :]
+            head = raw[j, :CHUNK, at].astype(f32)[:2]
             for t in range(2):
                 send_ref[modes + 2 * j + t, row, :] = rim[t : t + 1]
                 send_ref[modes + RIM + 2 * j + t, row, :] = head[t : t + 1]
@@ -163,14 +167,11 @@
 
     lax.fori_loop(0, groups, group, 0)
 
-    def landed(c, _):
-        fetch_query(c).wait()
-        rim = query_ref[c, tokens - TILE :, :].astype(f32)[TILE - 2 :]
+    fetch_query.wait()
+    for c in range(groups):
+        rim = query_ref[tokens - CHUNK :, lanes(c)].astype(f32)[CHUNK - 2 :]
         for t in range(2):
-            send_ref[modes + 4 + t, pl.ds(c, 1), :] = rim[t : t + 1]
-        return 0
-
-    lax.fori_loop(0, groups, landed, 0)
+            send_ref[modes + 4 + t, c : c + 1, :] = rim[t : t + 1]
 
 
 def join_kernel(size, tokens, last, tap_ref, rate_ref, coef_ref, skip_ref, other_ref, mine_ref, enter_ref, enter_out, *mine_out):
@@ -239,81 +240,94 @@
 
 
 def local_kernel(at, beside, query_ref, gated_ref, tap_ref, decay_ref, coef_ref, skip_ref, start_ref, *rest):
-    conv_ref, gate_ref, slots = rest[-3:]
+    conv_ref, gate_ref, *buffers = rest[-4:]
     steps = gated_ref.shape[1]
-    modes = decay_ref.shape[0]
+    modes, chunks = decay_ref.shape[0], steps // CHUNK
 
     def group(i, _):
         c = i + at
         on = lanes(c)
-        queries = Spread(query_ref.at[c], slots, steps)
+        queries = Spread(query_ref, c, buffers, steps)
         taps = [rows(tap_ref[d, 0:1, on]) for d in range(3)]
         decay = each(decay_ref, on)
         coef = [rows(coef_ref[n, pl.ds(c, 1), :]) for n in range(modes)]
         skip = rows(skip_ref[0, pl.ds(c, 1), :])
-        before = queries.begin()
-
-        def one(k, slot, u, carried):
+        queries.begin()
+        before = queries.before()
+
+        def one(k, side, u, carried):
             q1, q2, *state = carried
-            q0, x = queries.at(slot, u), gated_ref[c, k]
+            q0, x = queries.at(side, u), gated_ref[c, k]
             gate_ref[c, k] = taps[0] * q0 + taps[1] * q1 + taps[2] * q2
             state = [d * s + x for d, s in zip(decay, state)]
             conv_ref[c, k] = total([a * s for a, s in zip(coef, state)] + [skip * x])
             return (q0, q1, *state)
 
-        chunk_loop(steps, one, spreading((queries,)), (*before, *[start_ref[c, n] for n in range(modes)]))
+        def ahead(seg, chunk, side):
+            queries.load(seg, lax.rem(chunk + 1, chunks), side)
+
+        items = [(seg,) for seg in range(SEG)]
+        chunk_loop(steps, one, ahead, items, (*before, *[start_ref[c, n] for n in range(modes)]))
         return 0
 
     lax.fori_loop(0, beside, group, 0)
 
 
-def carry_kernel(conv_ref, gate_ref, rate_ref, decay_ref, enter_ref, out_ref, mixed, slots, sem):
+def carry_kernel(conv_ref, gate_ref, rate_ref, decay_ref, enter_ref, out_ref, mixed, *rest):
+    buffers, sem = rest[:2], rest[2]
     groups, steps = conv_ref.shape[:2]
-    modes, chunks = rate_ref.shape[0], steps // CHUNK
-
-    def store(c, side):
-        return pltpu.make_async_copy(mixed.at[side], out_ref.at[:, lanes(c)], sem.at[side])
+    modes = rate_ref.shape[0]
+    quarter = steps // 4
+
+    def store(c, side, part):
+        here = pl.ds(part * quarter, quarter)
+        return pltpu.make_async_copy(mixed.at[side, :, here, :], out_ref.at[:, here, lanes(c)], sem.at[side, part])
 
     def group(c, _):
-        side, on = lax.rem(c, 2), lanes(c)
+        half, on = lax.rem(c, 2), lanes(c)
 
         @pl.when(c >= 2)
         def _():
-            store(c - 2, side).wait()
+            for part in range(4):
+                store(c - 2, half, part).wait()
 
         row = pl.ds(c, 1)
         decay = each(decay_ref, on)
         first = lax.broadcasted_iota(jnp.int32, (SEG, LANES), 0).astype(f32) * steps
-        part = [jnp.exp(-rows(rate_ref[n : n + 1, on]) * first) * rows(enter_ref[n, row, :]) for n in range(modes)]
-
-        def one(k, slot, u, part):
+        start = [jnp.exp(-rows(rate_ref[n : n + 1, on]) * first) * rows(enter_ref[n, row, :]) for n in range(modes)]
+
+        def one(k, side, u, part):
             part = [d * s for d, s in zip(decay, part)]
-            slots[slot, pl.ds(u, SEG, stride=PITCH), :] = gate_ref[c, k] * (conv_ref[c, k] + total(part))
+            buffers[side][pl.ds(u, SEG, stride=PITCH), :] = gate_ref[c, k] * (conv_ref[c, k] + total(part))
             return part
 
-        def put(seg, chunk, slot, tile):
-            start = pl.multiple_of(seg * steps + chunk * CHUNK + tile * TILE, TILE)
-            mixed[side, pl.ds(start, TILE), :] = slots[slot, pl.ds(seg * PITCH + tile * TILE, TILE), :]
-
-        items = [(seg, tile) for tile in range(CHUNK // TILE) for seg in range(SEG)]
-
-        def ahead(u, b, coming, after):
-            for seg, tile in items[u * len(items) // CHUNK : (u + 1) * len(items) // CHUNK]:
-                put(seg, jnp.maximum(b - 1, 0), after, tile)
-
-        chunk_loop(steps, one, ahead, part)
-        for seg, tile in items:
-            put(seg, chunks - 1, (chunks - 1) % 2, tile)
-
-        for t in range(2):
-            gate = gate_ref[c, t, 0:1, :] + enter_ref[modes + 2 + t, row, :]
-            mixed[side, t : t + 1, :] = gate * (conv_ref[c, t, 0:1, :] + enter_ref[modes + t, row, :])
-        store(c, side).start()
+        def put(seg, chunk, side):
+            to = pl.ds(pl.multiple_of(chunk * CHUNK, CHUNK), CHUNK)
+            mixed[half, seg, to, :] = buffers[side][pl.ds(seg * PITCH, CHUNK), :]
+
+        def ahead(seg, chunk, side):
+            if side == 0:
+                put(seg, chunk - 1, side)
+
+        items = [(seg,) for seg in range(SEG)]
+        for part in range(4):
+            begin, end = part * quarter // (2 * CHUNK), (part + 1) * quarter // (2 * CHUNK)
+            start = chunk_loop(steps, one, ahead, items, start, begin, end)
+            for seg in range(SEG):
+                put(seg, 2 * end - 1, 1)
+            assert end == begin + 1
+            if part == 0:
+                for t in range(2):
+                    gate = gate_ref[c, t, 0:1, :] + enter_ref[modes + 2 + t, row, :]
+                    local = conv_ref[c, t, 0:1, :] + enter_ref[modes + t, row, :]
+                    mixed[half, 0, t : t + 1, :] = gate * local
+            store(c, half, part).start()
         return 0
 
     lax.fori_loop(0, groups, group, 0)
     for c in range(max(groups - 2, 0), groups):
-        store(c, c % 2).wait()
+        for part in range(4):
+            store(c, c % 2, part).wait()
 
 
 def in_hbm(x):
@@ -334,7 +348,7 @@
     steps = tokens // SEG
     groups = channels // LANES
     count = lax.axis_size("seq")
-    assert count & (count - 1) == 0 and tokens % (SEG * CHUNK * 2) == 0
+    assert count & (count - 1) == 0 and tokens % (SEG * CHUNK * 8) == 0
 
     by_stream = in_hbm(jnp.transpose(streams, (1, 0, 2)))
     apart = lax.optimization_barrier(rates)
@@ -343,8 +357,8 @@
     skip = skip.reshape(1, groups, LANES)
 
     segs = pltpu.VMEM((groups, steps, SEG, LANES), f32)
-    spread = pltpu.VMEM((2, SEG * CHUNK, LANES), f32)
-    slots = pltpu.VMEM((2, SEG * PITCH, LANES), f32)
+    spread = [pltpu.VMEM((SEG * CHUNK, LANES), f32)] * 2
+    gather = [pltpu.VMEM((SEG * PITCH, LANES), f32)] * 2
     hbm = pl.BlockSpec(memory_space=pltpu.HBM)
     whole = pl.BlockSpec(memory_space=pltpu.VMEM)
     params = pltpu.CompilerParams(vmem_limit_bytes=VMEM_LIMIT)
@@ -363,7 +377,7 @@
             segs,
             pltpu.VMEM((groups, modes, SEG, LANES), f32),
             tall(modes + RIM + HEAD),
-            pltpu.VMEM((groups, tokens, LANES), streams.dtype),
+            pltpu.VMEM((tokens, channels), streams.dtype),
             pltpu.VMEM(short_filter.shape, f32),
             tall(9),
             tall(modes),
@@ -372,12 +386,12 @@
             enter_shape,
         ],
         scratch_shapes=[
-            pltpu.VMEM((2, 2, tokens, LANES), streams.dtype),
+            pltpu.VMEM((2, tokens, channels), streams.dtype),
             mode_shape,
-            spread,
-            spread,
-            pltpu.SemaphoreType.DMA((2,)),
-            pltpu.SemaphoreType.DMA((groups,)),
+            *spread,
+            *spread,
+            pltpu.SemaphoreType.DMA((groups.bit_length(),)),
+            pltpu.SemaphoreType.DMA,
             pltpu.SemaphoreType.DMA((2,)),
         ],
         compiler_params=params,
@@ -397,7 +411,7 @@
                 out_specs=[whole] * 2,
                 out_shape=[segs, segs],
                 input_output_aliases={len(inputs) + i: i for i in range(len(made))},
-                scratch_shapes=[spread],
+                scratch_shapes=spread,
                 compiler_params=params,
                 name="local",
             )(*inputs, *made)
@@ -415,15 +429,16 @@
         block = None if last else blocks[0]
     conv, gate = made
 
-    return pl.pallas_call(
+    mixed = pl.pallas_call(
         carry_kernel,
         in_specs=[whole] * 5,
         out_specs=hbm,
-        out_shape=pltpu.HBM((tokens, channels), f32),
-        scratch_shapes=[pltpu.VMEM((2, tokens, LANES), f32), slots, pltpu.SemaphoreType.DMA((2,))],
+        out_shape=pltpu.HBM((SEG, steps, channels), f32),
+        scratch_shapes=[pltpu.VMEM((2, SEG, steps, LANES), f32), *gather, pltpu.SemaphoreType.DMA((2, 4))],
         compiler_params=params,
         name="carry",
     )(conv, gate, rate, decay, entering)
+    return mixed.reshape(tokens, channels)
 
 
 def solution(mesh):

time: 43.6 us -> 42.4 us (0.972)
  Pallas kernels: 27.9 us -> 26.8 us
    pallas_call x1, Pallas kernels: 9.41 us -> 8.84 us  [body(): pl.pallas_call(states_kernel, in_specs=[hbm] * 3, out_specs=[whole] * 10,...]
    pallas_call x1, Pallas kernels: 6.38 us -> 5.9 us  [body(): pl.pallas_call(carry_kernel, in_specs=[whole] * 5, out_specs=hbm, out_sha...]
  transfers between devices with their start and end apart: 4 -> 4, of which waited for: 3 -> 3; matrix products, arithmetic and copies ran while one was open for 0% -> 0% of each run, Pallas kernels for 27% -> 28%
where the time goes in v5:
time: 42.4 us; the launch traced here: 42.3 us
  Pallas kernels  26.8 us (63%)
  starting transfers between devices  8.23 us (19%)
  waiting for transfers between devices  7.11 us (17%)
    pallas_call x4, Pallas kernels, body(): pl.pallas_call(functools.partial(local_kernel, at, beside), in_specs=[who...  11.8 us
    pallas_call x1, Pallas kernels, body(): pl.pallas_call(states_kernel, in_specs=[hbm] * 3, out_specs=[whole] * 10,...  8.84 us
    ppermute x4, starting transfers between devices, body(): other = lax.ppermute(block, 'seq', [(i, i ^ size) for i in range(count)])  8.23 us
    ppermute x4, waiting for transfers between devices, body(): other = lax.ppermute(block, 'seq', [(i, i ^ size) for i in range(count)])  7.11 us
    pallas_call x1, Pallas kernels, body(): pl.pallas_call(carry_kernel, in_specs=[whole] * 5, out_specs=hbm, out_sha...  5.9 us
  transfers between devices with their start and end apart: 4, of which 3 were waited for; matrix products, arithmetic and copies ran while one was open for 0% of the time, Pallas kernels for 28%

profile of v5, /device:TPU:0, one launch (start us, length us, event | category | flops | bytes accessed | tf_op | source)
XLA Modules:
  0.0 42.3 jit_solution(9012406716527587303)
XLA Ops:
  0.0 0.0 copy-start.1
  0.0 0.0 copy-start.2
  0.0 0.0 copy-start
  0.0 8.8 %states.1 = (f32[8,128,8,128]{3,2,1,0:T(8,128)S(1)}, f32[8,16,8,128]{3,2,1,0:T(8,128)S(1)}, f32[26,8,128]{2,1,0:T(8,128)S(1)}, bf16[1024,1024]{1,0:T(8,128)(2,1)...) custom-call(bf16[3,1024,1024]{2,1,0:T(8,128)(2,1)} %bitcast.21, ...), custom_call_target="tpu_custom_call" | custom-call | tf_op jit(solution)/shard_map/states/pallas_call | solution.py:372
  8.8 0.6 %collective-permute-start = (f32[26,8,128]{2,1,0:T(8,128)S(1)}, f32[26,8,128]{2,1,0:T(8,128)S(1)}, u32[]{:S(2)}, u32[]{:S(2)}) collective-permute-start(f32[26,8,128]{2,1,0:T(8,128)S(1)} %get-tuple-element.45.mine_ref), channel_id=1, source_target_pairs={{0,1},{1,0},{2,3},{3,2},{4,5},{5,4},{6,7},{7,6},{8,9},{9,8},{10,11... | collective-permute-start | bytes 319496 | tf_op jit(solution)/shard_map/ppermute | solution.py:405
  9.4 0.0 copy-done.1
  9.4 0.0 copy-done.2
  9.5 0.9 %collective-permute-done.other_ref = f32[26,8,128]{2,1,0:T(8,128)S(1)} collective-permute-done((f32[26,8,128]{2,1,0:T(8,128)S(1)}, f32[26,8,128]{2,1,0:T(8,128)S(1)}, u32[]{:S(2)}, u32[]{:S(2)}) %collective-permute-start) | collective-permute-done | bytes 106528 | tf_op jit(solution)/shard_map/ppermute | solution.py:405
  10.4 0.0 copy-done
  10.4 0.1 join.4
  10.4 2.9 %collective-permute-start.1 = (f32[26,8,128]{2,1,0:T(8,128)S(1)}, f32[26,8,128]{2,1,0:T(8,128)S(1)}, u32[]{:S(2)}, u32[]{:S(2)}) collective-permute-start(f32[26,8,128]{2,1,0:T(8,128)S(1)} %get-tuple-element.47.mine_ref), channel_id=1, source_target_pairs={{0,2},{1,3},{2,0},{3,1},{4,6},{5,7},{6,4},{7,5},{8,10},{9,11},{10,... | collective-permute-start | bytes 319496 | tf_op jit(solution)/shard_map/ppermute | solution.py:405
  13.4 3.3 %collective-permute-done.1.other_ref = f32[26,8,128]{2,1,0:T(8,128)S(1)} collective-permute-done((f32[26,8,128]{2,1,0:T(8,128)S(1)}, f32[26,8,128]{2,1,0:T(8,128)S(1)}, u32[]{:S(2)}, u32[]{:S(2)}) %collective-permute-start.1) | collective-permute-done | bytes 106528 | tf_op jit(solution)/shard_map/ppermute | solution.py:405
  16.7 0.1 join.5
  16.7 1.9 %collective-permute-start.2 = (f32[26,8,128]{2,1,0:T(8,128)S(1)}, f32[26,8,128]{2,1,0:T(8,128)S(1)}, u32[]{:S(2)}, u32[]{:S(2)}) collective-permute-start(f32[26,8,128]{2,1,0:T(8,128)S(1)} %get-tuple-element.49.mine_ref), channel_id=1, source_target_pairs={{0,4},{1,5},{2,6},{3,7},{4,0},{5,1},{6,2},{7,3},{8,12},{9,13},{10,... | collective-permute-start | bytes 319496 | tf_op jit(solution)/shard_map/ppermute | solution.py:405
  18.6 2.9 %collective-permute-done.2.other_ref = f32[26,8,128]{2,1,0:T(8,128)S(1)} collective-permute-done((f32[26,8,128]{2,1,0:T(8,128)S(1)}, f32[26,8,128]{2,1,0:T(8,128)S(1)}, u32[]{:S(2)}, u32[]{:S(2)}) %collective-permute-start.2) | collective-permute-done | bytes 106528 | tf_op jit(solution)/shard_map/ppermute | solution.py:405
  21.5 0.1 join.6
  21.6 2.9 %collective-permute-start.3 = (f32[22,8,128]{2,1,0:T(8,128)S(1)}, f32[22,8,128]{2,1,0:T(8,128)S(1)}, u32[]{:S(2)}, u32[]{:S(2)}) collective-permute-start(f32[22,8,128]{2,1,0:T(8,128)S(1)} %get-tuple-element.51.mine_ref), channel_id=1, source_target_pairs={{0,8},{1,9},{2,10},{3,11},{4,12},{5,13},{6,14},{7,15},{8,0},{9,1},... | collective-permute-start | bytes 270344 | tf_op jit(solution)/shard_map/ppermute | solution.py:405
  24.4 1.5 %local.4 = (f32[8,128,8,128]{3,2,1,0:T(8,128)S(1)}, f32[8,128,8,128]{3,2,1,0:T(8,128)S(1)}) custom-call(bf16[1024,1024]{1,0:T(8,128)(2,1)S(1)} %get-tuple-element.29.query_ref, f32[8,128,8,128]{3,2,1,0:T(8,128)S(1)} %get-tuple-element.30.gated_ref, f32[3,3,1024]{2,1,0:T(4,128)S(1)} %get-tuple-element.31.tap_ref, f32[16,1024]{1,0:T(8,128)S(1)} %get-tuple-element.32.decay_ref, ...), custom_call_target="tpu_custom_call" | custom-call | tf_op jit(solution)/shard_map/local/pallas_call | solution.py:408
  25.9 4.5 %local.5 = (f32[8,128,8,128]{3,2,1,0:T(8,128)S(1)}, f32[8,128,8,128]{3,2,1,0:T(8,128)S(1)}) custom-call(bf16[1024,1024]{1,0:T(8,128)(2,1)S(1)} %get-tuple-element.29.query_ref, f32[8,128,8,128]{3,2,1,0:T(8,128)S(1)} %get-tuple-element.30.gated_ref, f32[3,3,1024]{2,1,0:T(4,128)S(1)} %get-tuple-element.31.tap_ref, ...), custom_call_target="tpu_custom_call", output_to_operand_aliasing={{0}: (7, {}), {1}: (8, {})} | custom-call | tf_op jit(solution)/shard_map/local/pallas_call | solution.py:408
  30.4 3.0 %local.6 = (f32[8,128,8,128]{3,2,1,0:T(8,128)S(1)}, f32[8,128,8,128]{3,2,1,0:T(8,128)S(1)}) custom-call(bf16[1024,1024]{1,0:T(8,128)(2,1)S(1)} %get-tuple-element.29.query_ref, f32[8,128,8,128]{3,2,1,0:T(8,128)S(1)} %get-tuple-element.30.gated_ref, f32[3,3,1024]{2,1,0:T(4,128)S(1)} %get-tuple-element.31.tap_ref, ...), custom_call_target="tpu_custom_call", output_to_operand_aliasing={{0}: (7, {}), {1}: (8, {})} | custom-call | tf_op jit(solution)/shard_map/local/pallas_call | solution.py:408
  33.3 3.0 %local.7 = (f32[8,128,8,128]{3,2,1,0:T(8,128)S(1)}, f32[8,128,8,128]{3,2,1,0:T(8,128)S(1)}) custom-call(bf16[1024,1024]{1,0:T(8,128)(2,1)S(1)} %get-tuple-element.29.query_ref, f32[8,128,8,128]{3,2,1,0:T(8,128)S(1)} %get-tuple-element.30.gated_ref, f32[3,3,1024]{2,1,0:T(4,128)S(1)} %get-tuple-element.31.tap_ref, ...), custom_call_target="tpu_custom_call", output_to_operand_aliasing={{0}: (7, {}), {1}: (8, {})} | custom-call | tf_op jit(solution)/shard_map/local/pallas_call | solution.py:408
  36.3 0.0 collective-permute-done.3.other_ref
  36.3 0.1 join.7.enter_ref
  36.4 5.9 %carry.1 = f32[8,128,1024]{2,1,0:T(8,128)} custom-call(f32[8,128,8,128]{3,2,1,0:T(8,128)S(1)} %get-tuple-element.40.conv_ref, f32[8,128,8,128]{3,2,1,0:T(8,128)S(1)} %get-tuple-element.41.gate_ref, f32[16,1024]{1,0:T(8,128)S(1)} %get-tuple-element.42.rate_ref, f32[16,1024]{1,0:T(8,128)S(1)} %get-tuple-element.32.decay_ref, f32[24,8,128]{2,1,0:T(8,128)S(1)} %join.7.enter_ref), custom_call_target="tpu_custom_call" | custom-call | tf_op jit(solution)/shard_map/carry/pallas_call | solution.py:432
  (2 shorter events, 0.1 us)
Async XLA Ops:
  0.0 9.4 %copy-start.1 = (f32[16,1024]{1,0:T(8,128)S(1)}, f32[16,1024]{1,0:T(8,128)}, u32[]{:S(2)}) copy-start(f32[16,1024]{1,0:T(8,128)} %rate_ref.1) | copy-start | bytes 196612
  0.0 9.4 %copy-start.2 = (f32[16,1024]{1,0:T(8,128)S(1)}, f32[16,1024]{1,0:T(8,128)}, u32[]{:S(2)}) copy-start(f32[16,1024]{1,0:T(8,128)} %param.7) | copy-start | bytes 196612
  0.0 10.4 %copy-start = (f32[1024]{0:T(1024)S(1)}, f32[1024]{0:T(1024)}, u32[]{:S(2)}) copy-start(f32[1024]{0:T(1024)} %param.9) | copy-start | bytes 12292
  8.8 1.5 %collective-permute-start = (f32[26,8,128]{2,1,0:T(8,128)S(1)}, f32[26,8,128]{2,1,0:T(8,128)S(1)}, u32[]{:S(2)}, u32[]{:S(2)}) collective-permute-start(f32[26,8,128]{2,1,0:T(8,128)S(1)} %get-tuple-element.45.mine_ref), channel_id=1, source_target_pairs={{0,1},{1,0},{2,3},{3,2},{4,5},{5,4},{6,7},{7,6},{8,9},{9,8},{10,11... | collective-permute-start | bytes 319496 | tf_op jit(solution)/shard_map/ppermute | solution.py:405
  10.4 6.2 %collective-permute-start.1 = (f32[26,8,128]{2,1,0:T(8,128)S(1)}, f32[26,8,128]{2,1,0:T(8,128)S(1)}, u32[]{:S(2)}, u32[]{:S(2)}) collective-permute-start(f32[26,8,128]{2,1,0:T(8,128)S(1)} %get-tuple-element.47.mine_ref), channel_id=1, source_target_pairs={{0,2},{1,3},{2,0},{3,1},{4,6},{5,7},{6,4},{7,5},{8,10},{9,11},{10,... | collective-permute-start | bytes 319496 | tf_op jit(solution)/shard_map/ppermute | solution.py:405
  16.7 4.8 %collective-permute-start.2 = (f32[26,8,128]{2,1,0:T(8,128)S(1)}, f32[26,8,128]{2,1,0:T(8,128)S(1)}, u32[]{:S(2)}, u32[]{:S(2)}) collective-permute-start(f32[26,8,128]{2,1,0:T(8,128)S(1)} %get-tuple-element.49.mine_ref), channel_id=1, source_target_pairs={{0,4},{1,5},{2,6},{3,7},{4,0},{5,1},{6,2},{7,3},{8,12},{9,13},{10,... | collective-permute-start | bytes 319496 | tf_op jit(solution)/shard_map/ppermute | solution.py:405
  21.6 14.7 %collective-permute-start.3 = (f32[22,8,128]{2,1,0:T(8,128)S(1)}, f32[22,8,128]{2,1,0:T(8,128)S(1)}, u32[]{:S(2)}, u32[]{:S(2)}) collective-permute-start(f32[22,8,128]{2,1,0:T(8,128)S(1)} %get-tuple-element.51.mine_ref), channel_id=1, source_target_pairs={{0,8},{1,9},{2,10},{3,11},{4,12},{5,13},{6,14},{7,15},{8,0},{9,1},... | collective-permute-start | bytes 270344 | tf_op jit(solution)/shard_map/ppermute | solution.py:405

commit v6 on v5

--- a/solution.py
+++ b/solution.py
@@ -335,10 +335,9 @@
 
 
 def windows(groups, rounds):
-    counts = [0] * rounds
-    order = [*range(1, rounds), 0]
-    for i in range(groups):
-        counts[order[i % rounds] if i < rounds else 1 + (i - rounds) % (rounds - 1)] += 1
+    counts = [(groups + r) // rounds for r in range(rounds)]
+    if counts[0] > 1 and rounds > 1:
+        counts[0], counts[-1] = counts[0] - 1, counts[-1] + 1
     return counts
 
 

time: 42.4 us -> 42.4 us (level)
  no operation moved by 1% of the time
where the time goes in v6:
time: 42.4 us; the launch traced here: 42.3 us
  Pallas kernels  26.8 us (63%)
  starting transfers between devices  8.23 us (19%)
  waiting for transfers between devices  7.11 us (17%)
    pallas_call x4, Pallas kernels, body(): pl.pallas_call(functools.partial(local_kernel, at, beside), in_specs=[who...  11.8 us
    pallas_call x1, Pallas kernels, body(): pl.pallas_call(states_kernel, in_specs=[hbm] * 3, out_specs=[whole] * 10,...  8.84 us
    ppermute x4, starting transfers between devices, body(): other = lax.ppermute(block, 'seq', [(i, i ^ size) for i in range(count)])  8.23 us
    ppermute x4, waiting for transfers between devices, body(): other = lax.ppermute(block, 'seq', [(i, i ^ size) for i in range(count)])  7.11 us
    pallas_call x1, Pallas kernels, body(): pl.pallas_call(carry_kernel, in_specs=[whole] * 5, out_specs=hbm, out_sha...  5.9 us
  transfers between devices with their start and end apart: 4, of which 3 were waited for; matrix products, arithmetic and copies ran while one was open for 0% of the time, Pallas kernels for 28%

profile of v6, /device:TPU:0, one launch (start us, length us, event | category | flops | bytes accessed | tf_op | source)
XLA Modules:
  0.0 42.3 jit_solution(8151555818904577571)
XLA Ops:
  0.0 0.0 copy-start.1
  0.0 0.0 copy-start.2
  0.0 0.0 copy-start
  0.0 8.8 %states.1 = (f32[8,128,8,128]{3,2,1,0:T(8,128)S(1)}, f32[8,16,8,128]{3,2,1,0:T(8,128)S(1)}, f32[26,8,128]{2,1,0:T(8,128)S(1)}, bf16[1024,1024]{1,0:T(8,128)(2,1)...) custom-call(bf16[3,1024,1024]{2,1,0:T(8,128)(2,1)} %bitcast.21, ...), custom_call_target="tpu_custom_call" | custom-call | tf_op jit(solution)/shard_map/states/pallas_call | solution.py:371
  8.8 0.6 %collective-permute-start = (f32[26,8,128]{2,1,0:T(8,128)S(1)}, f32[26,8,128]{2,1,0:T(8,128)S(1)}, u32[]{:S(2)}, u32[]{:S(2)}) collective-permute-start(f32[26,8,128]{2,1,0:T(8,128)S(1)} %get-tuple-element.45.mine_ref), channel_id=1, source_target_pairs={{0,1},{1,0},{2,3},{3,2},{4,5},{5,4},{6,7},{7,6},{8,9},{9,8},{10,11... | collective-permute-start | bytes 319496 | tf_op jit(solution)/shard_map/ppermute | solution.py:404
  9.4 0.0 copy-done.1
  9.4 0.0 copy-done.2
  9.5 0.9 %collective-permute-done.other_ref = f32[26,8,128]{2,1,0:T(8,128)S(1)} collective-permute-done((f32[26,8,128]{2,1,0:T(8,128)S(1)}, f32[26,8,128]{2,1,0:T(8,128)S(1)}, u32[]{:S(2)}, u32[]{:S(2)}) %collective-permute-start) | collective-permute-done | bytes 106528 | tf_op jit(solution)/shard_map/ppermute | solution.py:404
  10.4 0.0 copy-done
  10.4 0.1 join.4
  10.4 2.9 %collective-permute-start.1 = (f32[26,8,128]{2,1,0:T(8,128)S(1)}, f32[26,8,128]{2,1,0:T(8,128)S(1)}, u32[]{:S(2)}, u32[]{:S(2)}) collective-permute-start(f32[26,8,128]{2,1,0:T(8,128)S(1)} %get-tuple-element.47.mine_ref), channel_id=1, source_target_pairs={{0,2},{1,3},{2,0},{3,1},{4,6},{5,7},{6,4},{7,5},{8,10},{9,11},{10,... | collective-permute-start | bytes 319496 | tf_op jit(solution)/shard_map/ppermute | solution.py:404
  13.4 3.3 %collective-permute-done.1.other_ref = f32[26,8,128]{2,1,0:T(8,128)S(1)} collective-permute-done((f32[26,8,128]{2,1,0:T(8,128)S(1)}, f32[26,8,128]{2,1,0:T(8,128)S(1)}, u32[]{:S(2)}, u32[]{:S(2)}) %collective-permute-start.1) | collective-permute-done | bytes 106528 | tf_op jit(solution)/shard_map/ppermute | solution.py:404
  16.7 0.1 join.5
  16.7 1.9 %collective-permute-start.2 = (f32[26,8,128]{2,1,0:T(8,128)S(1)}, f32[26,8,128]{2,1,0:T(8,128)S(1)}, u32[]{:S(2)}, u32[]{:S(2)}) collective-permute-start(f32[26,8,128]{2,1,0:T(8,128)S(1)} %get-tuple-element.49.mine_ref), channel_id=1, source_target_pairs={{0,4},{1,5},{2,6},{3,7},{4,0},{5,1},{6,2},{7,3},{8,12},{9,13},{10,... | collective-permute-start | bytes 319496 | tf_op jit(solution)/shard_map/ppermute | solution.py:404
  18.6 2.9 %collective-permute-done.2.other_ref = f32[26,8,128]{2,1,0:T(8,128)S(1)} collective-permute-done((f32[26,8,128]{2,1,0:T(8,128)S(1)}, f32[26,8,128]{2,1,0:T(8,128)S(1)}, u32[]{:S(2)}, u32[]{:S(2)}) %collective-permute-start.2) | collective-permute-done | bytes 106528 | tf_op jit(solution)/shard_map/ppermute | solution.py:404
  21.5 0.1 join.6
  21.6 2.9 %collective-permute-start.3 = (f32[22,8,128]{2,1,0:T(8,128)S(1)}, f32[22,8,128]{2,1,0:T(8,128)S(1)}, u32[]{:S(2)}, u32[]{:S(2)}) collective-permute-start(f32[22,8,128]{2,1,0:T(8,128)S(1)} %get-tuple-element.51.mine_ref), channel_id=1, source_target_pairs={{0,8},{1,9},{2,10},{3,11},{4,12},{5,13},{6,14},{7,15},{8,0},{9,1},... | collective-permute-start | bytes 270344 | tf_op jit(solution)/shard_map/ppermute | solution.py:404
  24.4 1.5 %local.4 = (f32[8,128,8,128]{3,2,1,0:T(8,128)S(1)}, f32[8,128,8,128]{3,2,1,0:T(8,128)S(1)}) custom-call(bf16[1024,1024]{1,0:T(8,128)(2,1)S(1)} %get-tuple-element.29.query_ref, f32[8,128,8,128]{3,2,1,0:T(8,128)S(1)} %get-tuple-element.30.gated_ref, f32[3,3,1024]{2,1,0:T(4,128)S(1)} %get-tuple-element.31.tap_ref, f32[16,1024]{1,0:T(8,128)S(1)} %get-tuple-element.32.decay_ref, ...), custom_call_target="tpu_custom_call" | custom-call | tf_op jit(solution)/shard_map/local/pallas_call | solution.py:407
  25.9 3.0 %local.5 = (f32[8,128,8,128]{3,2,1,0:T(8,128)S(1)}, f32[8,128,8,128]{3,2,1,0:T(8,128)S(1)}) custom-call(bf16[1024,1024]{1,0:T(8,128)(2,1)S(1)} %get-tuple-element.29.query_ref, f32[8,128,8,128]{3,2,1,0:T(8,128)S(1)} %get-tuple-element.30.gated_ref, f32[3,3,1024]{2,1,0:T(4,128)S(1)} %get-tuple-element.31.tap_ref, ...), custom_call_target="tpu_custom_call", output_to_operand_aliasing={{0}: (7, {}), {1}: (8, {})} | custom-call | tf_op jit(solution)/shard_map/local/pallas_call | solution.py:407
  28.9 3.0 %local.6 = (f32[8,128,8,128]{3,2,1,0:T(8,128)S(1)}, f32[8,128,8,128]{3,2,1,0:T(8,128)S(1)}) custom-call(bf16[1024,1024]{1,0:T(8,128)(2,1)S(1)} %get-tuple-element.29.query_ref, f32[8,128,8,128]{3,2,1,0:T(8,128)S(1)} %get-tuple-element.30.gated_ref, f32[3,3,1024]{2,1,0:T(4,128)S(1)} %get-tuple-element.31.tap_ref, ...), custom_call_target="tpu_custom_call", output_to_operand_aliasing={{0}: (7, {}), {1}: (8, {})} | custom-call | tf_op jit(solution)/shard_map/local/pallas_call | solution.py:407
  31.9 4.4 %local.7 = (f32[8,128,8,128]{3,2,1,0:T(8,128)S(1)}, f32[8,128,8,128]{3,2,1,0:T(8,128)S(1)}) custom-call(bf16[1024,1024]{1,0:T(8,128)(2,1)S(1)} %get-tuple-element.29.query_ref, f32[8,128,8,128]{3,2,1,0:T(8,128)S(1)} %get-tuple-element.30.gated_ref, f32[3,3,1024]{2,1,0:T(4,128)S(1)} %get-tuple-element.31.tap_ref, ...), custom_call_target="tpu_custom_call", output_to_operand_aliasing={{0}: (7, {}), {1}: (8, {})} | custom-call | tf_op jit(solution)/shard_map/local/pallas_call | solution.py:407
  36.3 0.0 collective-permute-done.3.other_ref
  36.3 0.1 join.7.enter_ref
  36.4 5.9 %carry.1 = f32[8,128,1024]{2,1,0:T(8,128)} custom-call(f32[8,128,8,128]{3,2,1,0:T(8,128)S(1)} %get-tuple-element.40.conv_ref, f32[8,128,8,128]{3,2,1,0:T(8,128)S(1)} %get-tuple-element.41.gate_ref, f32[16,1024]{1,0:T(8,128)S(1)} %get-tuple-element.42.rate_ref, f32[16,1024]{1,0:T(8,128)S(1)} %get-tuple-element.32.decay_ref, f32[24,8,128]{2,1,0:T(8,128)S(1)} %join.7.enter_ref), custom_call_target="tpu_custom_call" | custom-call | tf_op jit(solution)/shard_map/carry/pallas_call | solution.py:431
  (2 shorter events, 0.1 us)
Async XLA Ops:
  0.0 9.4 %copy-start.1 = (f32[16,1024]{1,0:T(8,128)S(1)}, f32[16,1024]{1,0:T(8,128)}, u32[]{:S(2)}) copy-start(f32[16,1024]{1,0:T(8,128)} %rate_ref.1) | copy-start | bytes 196612
  0.0 9.4 %copy-start.2 = (f32[16,1024]{1,0:T(8,128)S(1)}, f32[16,1024]{1,0:T(8,128)}, u32[]{:S(2)}) copy-start(f32[16,1024]{1,0:T(8,128)} %param.7) | copy-start | bytes 196612
  0.0 10.4 %copy-start = (f32[1024]{0:T(1024)S(1)}, f32[1024]{0:T(1024)}, u32[]{:S(2)}) copy-start(f32[1024]{0:T(1024)} %param.9) | copy-start | bytes 12292
  8.8 1.5 %collective-permute-start = (f32[26,8,128]{2,1,0:T(8,128)S(1)}, f32[26,8,128]{2,1,0:T(8,128)S(1)}, u32[]{:S(2)}, u32[]{:S(2)}) collective-permute-start(f32[26,8,128]{2,1,0:T(8,128)S(1)} %get-tuple-element.45.mine_ref), channel_id=1, source_target_pairs={{0,1},{1,0},{2,3},{3,2},{4,5},{5,4},{6,7},{7,6},{8,9},{9,8},{10,11... | collective-permute-start | bytes 319496 | tf_op jit(solution)/shard_map/ppermute | solution.py:404
  10.4 6.2 %collective-permute-start.1 = (f32[26,8,128]{2,1,0:T(8,128)S(1)}, f32[26,8,128]{2,1,0:T(8,128)S(1)}, u32[]{:S(2)}, u32[]{:S(2)}) collective-permute-start(f32[26,8,128]{2,1,0:T(8,128)S(1)} %get-tuple-element.47.mine_ref), channel_id=1, source_target_pairs={{0,2},{1,3},{2,0},{3,1},{4,6},{5,7},{6,4},{7,5},{8,10},{9,11},{10,... | collective-permute-start | bytes 319496 | tf_op jit(solution)/shard_map/ppermute | solution.py:404
  16.7 4.8 %collective-permute-start.2 = (f32[26,8,128]{2,1,0:T(8,128)S(1)}, f32[26,8,128]{2,1,0:T(8,128)S(1)}, u32[]{:S(2)}, u32[]{:S(2)}) collective-permute-start(f32[26,8,128]{2,1,0:T(8,128)S(1)} %get-tuple-element.49.mine_ref), channel_id=1, source_target_pairs={{0,4},{1,5},{2,6},{3,7},{4,0},{5,1},{6,2},{7,3},{8,12},{9,13},{10,... | collective-permute-start | bytes 319496 | tf_op jit(solution)/shard_map/ppermute | solution.py:404
  21.6 14.7 %collective-permute-start.3 = (f32[22,8,128]{2,1,0:T(8,128)S(1)}, f32[22,8,128]{2,1,0:T(8,128)S(1)}, u32[]{:S(2)}, u32[]{:S(2)}) collective-permute-start(f32[22,8,128]{2,1,0:T(8,128)S(1)} %get-tuple-element.51.mine_ref), channel_id=1, source_target_pairs={{0,8},{1,9},{2,10},{3,11},{4,12},{5,13},{6,14},{7,15},{8,0},{9,1},... | collective-permute-start | bytes 270344 | tf_op jit(solution)/shard_map/ppermute | solution.py:404
